TPU v7x, 256 devices: a whole 4x4x8 slice. The times are simulated.
256 devices in a mesh: seq: 64 (over z, y, core), head: 4 (over x).
Axes of the slice: x: 4, y: 4, z: 8, core: 2. Of those that a mesh axis runs over, the one named last changes fastest.
Arguments:
- tokens: bfloat16 [16384, 4096], P('seq', 'head'), may hold values from -6 to 6
- light_input: bfloat16 [3, 4096, 1024], P(None, None, 'head'), may hold values from -14 to 14
- light_output: bfloat16 [1024, 4096], P('head'), may hold values from -0.75 to 0.75
- heavy_input: bfloat16 [3, 4096, 4096], P(None, 'seq', 'head'), may hold values from -14 to 14
- heavy_output: bfloat16 [4096, 4096], P('head', 'seq'), may hold values from -0.75 to 0.75
- query_tokens: int32 [64, 32], replicated, may hold values from -1 to 255, as said below
- context_tokens: int32 [64, 32], replicated, may hold values from -1 to 255, as said below
- query_gate: float32 [64, 32], P('seq'), may hold values from 0.25 to 2
Outputs:
- mixed: bfloat16 [16384, 4096], P('seq', 'head')
Inputs may be any that keep to these rules, and one draw needn't show every extreme that they name: `query_tokens`: row s lists, in its first entries, distinct positions within sequence shard s of routed query tokens, and -1 after them; 512 positions are listed over all rows, at most 32 in a row, and exactly 32 in some row. `context_tokens`: row s lists, in its first entries, distinct positions within sequence shard s of routed key-value tokens, and -1 after them; 512 positions are listed over all rows, at most 32 in a row, and exactly 32 in some row.
All inputs are finite; a program needn't handle non-finite values.
Results may differ from a plain program's by a relative error of at most 0.012.
Values may be sent and summed in bfloat16 or wider, within the bound.
A program may use at most 64 MiB of HBM per device.

v0:
```python
import math

import jax
import jax.numpy as jnp
from jax import lax
from jax.sharding import PartitionSpec as P

HD = 128
LB = 128
ROUTE = 32


def sent_together(arrays, axis, dim, along):
    ends, at = ([], 0)
    for a in arrays[:-1]:
        at += a.shape[along]
        ends.append(at)
    both = jnp.concatenate(arrays, axis=along)
    return tuple(jnp.split(lax.all_gather(both, axis, axis=dim, tiled=True), ends, axis=along))


def copy_for_each(shard, axis):
    copies = jnp.broadcast_to(shard, (lax.axis_size(axis), *shard.shape))
    return lax.all_to_all(copies, axis, split_axis=0, concat_axis=0, tiled=True)


def joined_along(pieces, dim):
    shape = list(pieces.shape[1:])
    shape[dim] *= pieces.shape[0]
    return jnp.moveaxis(pieces, 0, dim).reshape(shape)


def gather_directly(shard, axis, dim):
    pieces = copy_for_each(shard, axis)
    return joined_along(pieces, dim)


def cut_along(shard, dim, peers):
    before, after = (shard.shape[:dim], shard.shape[dim + 1 :])
    return jnp.moveaxis(shard.reshape(*before, peers, -1, *after), dim, 0)


def sent_and_summed(shard, axis, dim):
    pieces = cut_along(shard, dim, lax.axis_size(axis))
    arrived = lax.all_to_all(pieces, axis, split_axis=0, concat_axis=0, tiled=True)
    return arrived.astype(jnp.float32).sum(axis=0)


def attend(queries, key_rows, value_rows):
    scores = jnp.einsum(
        "bqhe,bkhe->bhqk", queries, key_rows, preferred_element_type=jnp.float32
    ) / math.sqrt(queries.shape[-1])
    highest = jnp.max(scores, axis=-1, keepdims=True)
    expanded = jnp.exp(scores - highest)
    totals = jnp.sum(expanded, axis=-1)
    weighted = jnp.einsum(
        "bhqk,bkhe->bqhe",
        expanded.astype(jnp.bfloat16),
        value_rows,
        preferred_element_type=jnp.float32,
    )
    return (weighted / jnp.transpose(totals, (0, 2, 1))[..., None]).astype(jnp.bfloat16)


def routed_map(table, routed):
    counts = jnp.sum((table >= 0).astype(jnp.int32), axis=1)
    upper_end = jnp.cumsum(counts)
    lower_end = upper_end - counts
    compact_rows = jnp.arange(routed, dtype=jnp.int32)
    source_shard = jnp.sum((upper_end[None, :] <= compact_rows[:, None]).astype(jnp.int32), axis=1)
    onehot_shard = (
        source_shard[:, None] == jnp.arange(table.shape[0], dtype=jnp.int32)[None, :]
    ).astype(jnp.int32)
    within = compact_rows - jnp.sum(onehot_shard * lower_end[None, :], axis=1)
    return (source_shard * table.shape[1] + within, lower_end)


def project(query_part, source_part, weights):
    stacked = jnp.stack((query_part, source_part, source_part))
    return jnp.einsum("cmd,cdw->mcw", stacked, weights, preferred_element_type=jnp.float32)


def pick_rows(gathered, own_list):
    chosen = jnp.take(gathered, jnp.maximum(own_list, 0), axis=0)
    return jnp.where((own_list >= 0)[:, None], chosen, jnp.zeros_like(chosen))


def body(
    tokens,
    light_input,
    light_output,
    heavy_input,
    heavy_output,
    query_tokens,
    context_tokens,
    query_gate,
):
    gathered = lax.all_gather(tokens, "head", axis=1, tiled=True)
    tok_rows = gathered.shape[0]
    light_mapped = jnp.einsum(
        "td,cdw->ctw", gathered, light_input, preferred_element_type=jnp.float32
    ).astype(jnp.bfloat16)
    light_blocks = light_mapped.reshape(3, tok_rows // LB, LB, -1, HD)
    light_heads = attend(light_blocks[0], light_blocks[1], light_blocks[2]).reshape(tok_rows, -1)
    every_head = lax.all_gather(light_heads, "head", axis=1, tiled=True)
    column_weights = lax.all_to_all(light_output, "head", split_axis=1, concat_axis=0, tiled=True)
    light_part = jnp.dot(every_head, column_weights, preferred_element_type=jnp.float32)
    seq_count = lax.axis_size("seq")
    routed = seq_count * tok_rows // ROUTE
    slot_count = query_tokens.shape[1]
    seq_index = lax.axis_index("seq")
    own_queries = lax.dynamic_index_in_dim(query_tokens, seq_index, 0, keepdims=False)
    own_sources = lax.dynamic_index_in_dim(context_tokens, seq_index, 0, keepdims=False)
    query_cols, source_cols = (
        lax.all_to_all(
            pick_rows(gathered, own_queries), "seq", split_axis=1, concat_axis=0, tiled=True
        ),
        lax.all_to_all(
            pick_rows(gathered, own_sources), "seq", split_axis=1, concat_axis=0, tiled=True
        ),
    )
    query_index, query_lower = routed_map(query_tokens, routed)
    source_index = routed_map(context_tokens, routed)[0]
    query_rows = jnp.take(query_cols, query_index, axis=0)
    source_rows = jnp.take(source_cols, source_index, axis=0)
    per_device = routed // seq_count
    owned = lax.psum_scatter(
        project(query_rows, source_rows, heavy_input), "seq", scatter_dimension=0, tiled=True
    ).astype(jnp.bfloat16)
    local_queries = owned[:, 0].reshape(per_device, -1, HD)
    head_count = local_queries.shape[1]
    pieces = sent_together((owned[:, 1], owned[:, 2]), "seq", 0, 1)
    highest = jnp.full((head_count, per_device), -1e30, jnp.float32)
    key_rows = pieces[0].reshape(pieces[0].shape[0], head_count, HD)
    value_rows = pieces[1].reshape(pieces[1].shape[0], head_count, HD)
    scores = jnp.einsum(
        "qhe,khe->hqk", local_queries, key_rows, preferred_element_type=jnp.float32
    ) / math.sqrt(HD)
    raised = jnp.maximum(highest, jnp.max(scores, axis=-1))
    expanded = jnp.exp(scores - raised[..., None])
    totals = jnp.sum(expanded, axis=-1)
    weighted = jnp.einsum(
        "hqk,khe->qhe",
        expanded.astype(jnp.bfloat16),
        value_rows,
        preferred_element_type=jnp.float32,
    )
    highest, totals, weighted = (raised, totals, weighted)
    local_heads = (
        (weighted / jnp.transpose(totals)[..., None]).astype(jnp.bfloat16).reshape(per_device, -1)
    )
    heavy_part = jnp.dot(
        gather_directly(local_heads, "seq", 0), heavy_output, preferred_element_type=jnp.float32
    )
    slot_live = query_tokens >= 0
    compact = query_lower[:, None] + jnp.arange(slot_count, dtype=jnp.int32)[None, :]
    outgoing = jnp.take(heavy_part, jnp.where(slot_live, compact, 0).reshape(-1), axis=0)
    outgoing = jnp.where(slot_live.reshape(-1)[:, None], outgoing, jnp.zeros_like(outgoing))
    returned = lax.all_to_all(
        outgoing.astype(jnp.bfloat16), "seq", split_axis=0, concat_axis=1, tiled=True
    ).astype(outgoing.dtype)
    scaled = returned * query_gate[0][:, None]
    targets = jnp.where(own_queries >= 0, own_queries, tok_rows)
    heavy_columns = sent_and_summed(scaled.astype(jnp.bfloat16), "head", 1)
    return light_part.at[targets].add(heavy_columns, mode="drop").astype(jnp.bfloat16)


def solution(mesh):
    placed = (
        P("seq", "head"),
        P(None, None, "head"),
        P("head", None),
        P(None, "seq", "head"),
        P("head", "seq"),
        P(),
        P(),
        P("seq", None),
    )
    return jax.shard_map(
        body, mesh=mesh, in_specs=placed, out_specs=P("seq", "head"), check_vma=False
    )
```

profile of v0, /device:TPU:1, one launch (start us, length us, event | category | flops | bytes accessed | tf_op | source)
XLA Modules:
  0.0 409.7 jit_solution(3372663867552621975)
XLA Ops:
  6.5 0.7 all-gather.3.cloned.1.call-update
  7.3 0.7 convert_reduce_fusion.3
  8.3 1.3 convert_reduce_fusion.4
  10.0 0.9 maximum_reduce_fusion
  10.9 1.4 maximum_reduce_fusion.1
  12.3 1.5 compare_reduce_fusion
  14.1 0.5 compare_and_fusion.2
  14.7 0.5 compare_and_fusion.1
  15.2 31.2 %all-gather.3.cloned.1.call-done = bf16[256,4096]{1,0:T(8,128)(2,1)} async-done(((bf16[256,1024]{1,0:T(8,128)(2,1)}), bf16[256,4096]{1,0:T(8,128)(2,1)}) %all-gather.3.cloned.1.call-update) | async-done | bytes 2097168 | tf_op jit(solution)/shard_map/all_gather | solution.py:98
  46.4 2.8 gather_fusion.3
  49.3 0.5 all_to_all.64
  49.9 0.3 copy.135
  50.2 1.0 reshape.288
  51.3 10.9 %all-to-all-start.2 = ((bf16[64,2,1024]{2,1,0:T(2,128)(2,1)}), bf16[64,2,1024]{2,1,0:T(2,128)(2,1)}, u32[]{:S(2)}, u32[]{:S(2)}) async-start(bf16[64,2,1024]{2,1,0:T(2,128)(2,1)} %reshape.288), calls=%async_computation.2 | async-start | bytes 524288 | tf_op jit(solution)/shard_map/all_to_all | solution.py:118
  62.2 0.7 gather_fusion.1
  63.0 0.5 all_to_all.60
  63.5 0.3 copy.136
  63.9 1.0 reshape.290
  64.9 10.3 %all-to-all-done.2 = bf16[64,2,1024]{2,1,0:T(2,128)(2,1)} async-done(((bf16[64,2,1024]{2,1,0:T(2,128)(2,1)}), bf16[64,2,1024]{2,1,0:T(2,128)(2,1)}, u32[]{:S(2)}, u32[]{:S(2)}) %all-to-all-start.2) | async-done | bytes 262176 | tf_op jit(solution)/shard_map/all_to_all | solution.py:118
  75.2 4.7 %all-to-all-start.1 = ((bf16[64,2,1024]{2,1,0:T(2,128)(2,1)}), bf16[64,2,1024]{2,1,0:T(2,128)(2,1)S(1)}, u32[]{:S(2)}, u32[]{:S(2)}) async-start(bf16[64,2,1024]{2,1,0:T(2,128)(2,1)} %reshape.290), calls=%async_computation.1 | async-start | bytes 524288 | tf_op jit(solution)/shard_map/all_to_all | solution.py:115
  80.1 1.3 reshape.289
  81.5 1.3 gather_fusion.4
  82.9 10.2 %all-to-all-done.1 = bf16[64,2,1024]{2,1,0:T(2,128)(2,1)S(1)} async-done(((bf16[64,2,1024]{2,1,0:T(2,128)(2,1)}), bf16[64,2,1024]{2,1,0:T(2,128)(2,1)S(1)}, u32[]{:S(2)}, u32[]{:S(2)}) %all-to-all-start.1) | async-done | bytes 262176 | tf_op jit(solution)/shard_map/all_to_all | solution.py:115
  93.1 0.3 reshape.291
  93.4 1.3 gather_fusion.2
  95.0 3.7 convolution_bitcast_fusion
  98.7 136.8 %reduce-scatter.2.cloned.1.call-done = f32[8,3,1024]{2,0,1:T(8,128)} async-done(((f32[512,3,1024]{2,0,1:T(8,128)}), f32[8,3,1024]{2,0,1:T(8,128)}) %reduce-scatter.2.cloned.1.call-update) | async-done | bytes 98320 | tf_op jit(solution)/shard_map/reduce_scatter | solution.py:127
  235.5 0.9 convert_element_type.67
  236.4 0.6 pad_maximum_fusion
  237.1 4.1 copy.89
  241.2 4.6 %all-to-all-start = ((bf16[256,4,1024]{0,2,1:T(8,128)(2,1)}), bf16[256,4,1024]{0,2,1:T(8,128)(2,1)}, u32[]{:S(2)}, u32[]{:S(2)}) async-start(bf16[256,4,1024]{0,2,1:T(8,128)(2,1)} %bitcast.104), calls=%async_computation | async-start | bytes 4194304 | tf_op jit(solution)/shard_map/all_to_all | solution.py:106
  245.8 73.9 %all-gather.5.cloned.1.call-done = bf16[512,2048]{1,0:T(8,128)(2,1)} async-done(((bf16[8,2048]{1,0:T(8,128)(2,1)}), bf16[512,2048]{1,0:T(8,128)(2,1)}) %all-gather.5.cloned.1.call-update) | async-done | bytes 2097168 | tf_op jit(solution)/shard_map/all_gather | solution.py:19
  319.7 1.7 slice_bitcast_fusion
  321.4 0.5 fusion.40
  322.0 0.3 fusion.12
  322.4 1.1 broadcast_in_dim.89
  323.5 6.6 %all-to-all-start.3 = ((bf16[64,8,1024]{2,1,0:T(8,128)(2,1)}), bf16[64,8,1024]{2,1,0:T(8,128)(2,1)S(1)}, u32[]{:S(2)}, u32[]{:S(2)}) async-start(bf16[64,8,1024]{2,1,0:T(8,128)(2,1)} %broadcast_in_dim.89), calls=%async_computation.4 | async-start | bytes 2097152 | tf_op jit(solution)/shard_map/all_to_all | solution.py:24
  330.1 1.3 compare_and_fusion
  331.4 1.4 copy.91
  332.8 0.7 copy.101
  333.5 0.8 reshape.218
  334.3 0.8 copy.93
  335.1 1.2 fusion.36
  336.3 4.0 copy.90
  340.3 4.6 %fusion.5 = bf16[3,256,256]{1,2,0:T(8,128)(2,1)S(1)} fusion(bf16[3,4096,256]{2,1,0:T(8,128)(2,1)} %param.13, bf16[256,4096]{1,0:T(8,128)(2,1)S(1)} %copy-done.1), kind=kOutput, calls=%fused_computation.10 | convolution fusion | flops 1610809344 | bytes 8781824 | tf_op jit(solution)/shard_map/td,cdw->ctw/dot_general | solution.py:100
  345.3 12.8 %all-to-all-done.3 = bf16[64,8,1024]{2,1,0:T(8,128)(2,1)S(1)} async-done(((bf16[64,8,1024]{2,1,0:T(8,128)(2,1)}), bf16[64,8,1024]{2,1,0:T(8,128)(2,1)S(1)}, u32[]{:S(2)}, u32[]{:S(2)}) %all-to-all-start.3) | async-done | bytes 1048608 | tf_op jit(solution)/shard_map/all_to_all | solution.py:24
  358.1 0.4 fusion.17
  358.5 6.2 %gather_fusion = bf16[2048,64]{1,0:T(8,128)(2,1)S(1)} fusion(bf16[512,64]{1,0:T(8,128)(2,1)S(1)} %fusion.17, s32[2048]{0:T(1024)S(1)} %broadcast_clamp_fusion), kind=kCustom, calls=%fused_computation.4 | custom fusion | bytes 532480 | tf_op jit(solution)/shard_map/jit(_take)/gather | solution.py:157
  364.7 0.7 select_convert_fusion
  365.5 1.0 reshape.292
  366.5 6.5 %all-to-all-start.4 = ((bf16[64,2,1024]{2,1,0:T(2,128)(2,1)}), bf16[64,2,1024]{2,1,0:T(2,128)(2,1)S(1)}, u32[]{:S(2)}, u32[]{:S(2)}) async-start(bf16[64,2,1024]{2,1,0:T(2,128)(2,1)} %reshape.292), calls=%async_computation.5 | async-start | bytes 524288 | tf_op jit(solution)/shard_map/all_to_all | solution.py:159
  373.4 11.6 %all_gather.10 = bf16[256,1024]{1,0:T(8,128)(2,1)} all-gather(bf16[256,256]{1,0:T(8,128)(2,1)S(1)} %bitcast.110), channel_id=1, replica_groups=mesh['seq'=64,'head'=4] {'head'}, dimensions={1}, use_global_device_ids=true | all-gather | bytes 655360 | tf_op jit(solution)/shard_map/all_gather | solution.py:105
  385.0 1.1 all-to-all-done.4
  386.1 0.3 reshape.293
  386.6 0.6 copy.103
  387.2 1.2 reshape.219
  388.4 1.2 fusion.19
  389.6 0.8 copy.104
  390.4 4.0 all-to-all-start.5
  394.5 1.7 fusion.41
  396.3 3.8 all-to-all-done.5
  400.1 1.0 convert_reduce_fusion
  401.1 1.3 scatter_fusion
  402.3 0.9 convert_element_type.76
  (72 shorter events, 2.8 us)
Async XLA Ops:
  6.5 88.4 %copy-start = (bf16[3,64,1024]{2,1,0:T(8,128)(2,1)S(1)}, bf16[3,64,1024]{2,1,0:T(8,128)(2,1)}, u32[]{:S(2)}) copy-start(bf16[3,64,1024]{2,1,0:T(8,128)(2,1)} %param.15) | copy-start | bytes 1179652
  6.5 39.8 %all-gather.3.cloned.1.call-start = ((), (), s32[]{:S(2)}) async-start(), calls=%async_computation.7 | async-start | bytes 2621440 | tf_op jit(solution)/shard_map/all_gather | solution.py:98
  10.0 70.0 %copy-start.6 = (s32[64]{0:T(128)}, s32[64]{0:T(128)S(1)}, u32[]{:S(2)}) copy-start(s32[64]{0:T(128)S(1)} %sub.42) | copy-start | bytes 772
  49.2 12.9 %copy-start.1 = (bf16[256,4096]{1,0:T(8,128)(2,1)S(1)}, bf16[256,4096]{1,0:T(8,128)(2,1)}, u32[]{:S(2)}) copy-start(bf16[256,4096]{1,0:T(8,128)(2,1)} %all-gather.3.cloned.1.call-done) | copy-start | bytes 6291460
  50.2 12.6 %copy-start.9 = (pred[32]{0:T(512)(128)(4,1)S(1)}, pred[32]{0:T(512)(128)(4,1)}, u32[]{:S(2)}) copy-start(pred[32]{0:T(512)(128)(4,1)} %get-tuple-element.31) | copy-start | bytes 100
  50.2 12.6 %copy-start.10 = (pred[32]{0:T(512)(128)(4,1)S(1)}, pred[32]{0:T(512)(128)(4,1)}, u32[]{:S(2)}) copy-start(pred[32]{0:T(512)(128)(4,1)} %get-tuple-element.29) | copy-start | bytes 100
  51.3 24.0 %all-to-all-start.2 = ((bf16[64,2,1024]{2,1,0:T(2,128)(2,1)}), bf16[64,2,1024]{2,1,0:T(2,128)(2,1)}, u32[]{:S(2)}, u32[]{:S(2)}) async-start(bf16[64,2,1024]{2,1,0:T(2,128)(2,1)} %reshape.288), calls=%async_computation.2 | async-start | bytes 524288 | tf_op jit(solution)/shard_map/all_to_all | solution.py:118
  75.2 17.9 %all-to-all-start.1 = ((bf16[64,2,1024]{2,1,0:T(2,128)(2,1)}), bf16[64,2,1024]{2,1,0:T(2,128)(2,1)S(1)}, u32[]{:S(2)}, u32[]{:S(2)}) async-start(bf16[64,2,1024]{2,1,0:T(2,128)(2,1)} %reshape.290), calls=%async_computation.1 | async-start | bytes 524288 | tf_op jit(solution)/shard_map/all_to_all | solution.py:115
  79.9 155.6 %reduce-scatter.2.cloned.1.call-start = ((), (), s32[]{:S(2)}) async-start(), calls=%async_computation.8 | async-start | bytes 6389760 | tf_op jit(solution)/shard_map/reduce_scatter | solution.py:127
  80.1 14.8 %copy-start.8 = (pred[512]{0:T(512)(128)(4,1)S(1)}, pred[512]{0:T(512)(128)(4,1)}, u32[]{:S(2)}) copy-start(pred[512]{0:T(512)(128)(4,1)} %get-tuple-element.13) | copy-start | bytes 1540
  98.7 221.0 %all-gather.5.cloned.1.call-start = ((), (), s32[]{:S(2)}) async-start(), calls=%async_computation.9 | async-start | bytes 2129920 | tf_op jit(solution)/shard_map/all_gather | solution.py:19
  241.2 4.6 %copy-start.4 = (pred[64,32]{0,1:T(8,128)(4,1)S(1)}, pred[64,32]{0,1:T(8,128)(4,1)}, u32[]{:S(2)}) copy-start(pred[64,32]{0,1:T(8,128)(4,1)} %get-tuple-element.12) | copy-start | bytes 6148
  241.2 4.6 %copy-start.7 = (s32[64]{0:T(128)S(1)}, s32[64]{0:T(128)}, u32[]{:S(2)}) copy-start(s32[64]{0:T(128)} %copy-done.6) | copy-start | bytes 772
  241.2 81.2 %all-to-all-start = ((bf16[256,4,1024]{0,2,1:T(8,128)(2,1)}), bf16[256,4,1024]{0,2,1:T(8,128)(2,1)}, u32[]{:S(2)}, u32[]{:S(2)}) async-start(bf16[256,4,1024]{0,2,1:T(8,128)(2,1)} %bitcast.104), calls=%async_computation | async-start | bytes 4194304 | tf_op jit(solution)/shard_map/all_to_all | solution.py:106
  323.5 34.6 %all-to-all-start.3 = ((bf16[64,8,1024]{2,1,0:T(8,128)(2,1)}), bf16[64,8,1024]{2,1,0:T(8,128)(2,1)S(1)}, u32[]{:S(2)}, u32[]{:S(2)}) async-start(bf16[64,8,1024]{2,1,0:T(8,128)(2,1)} %broadcast_in_dim.89), calls=%async_computation.4 | async-start | bytes 2097152 | tf_op jit(solution)/shard_map/all_to_all | solution.py:24
  344.9 13.2 %copy-start.3 = (bf16[1024,64]{0,1:T(8,128)(2,1)S(1)}, bf16[1024,64]{0,1:T(8,128)(2,1)}, u32[]{:S(2)}) copy-start(bf16[1024,64]{0,1:T(8,128)(2,1)} %param.16) | copy-start | bytes 393220
  358.5 6.2 %copy-start.5 = (pred[64,32]{1,0:T(8,128)(4,1)S(1)}, pred[64,32]{1,0:T(8,128)(4,1)}, u32[]{:S(2)}) copy-start(pred[64,32]{1,0:T(8,128)(4,1)} %copy.91) | copy-start | bytes 6148
  366.5 19.6 %all-to-all-start.4 = ((bf16[64,2,1024]{2,1,0:T(2,128)(2,1)}), bf16[64,2,1024]{2,1,0:T(2,128)(2,1)S(1)}, u32[]{:S(2)}, u32[]{:S(2)}) async-start(bf16[64,2,1024]{2,1,0:T(2,128)(2,1)} %reshape.292), calls=%async_computation.5 | async-start | bytes 524288 | tf_op jit(solution)/shard_map/all_to_all | solution.py:159
  386.6 1.9 copy-start.12
  387.2 7.3 %copy-start.2 = (bf16[4,256,1024]{2,1,0:T(8,128)(2,1)S(1)}, bf16[4,256,1024]{2,1,0:T(8,128)(2,1)}, u32[]{:S(2)}) copy-start(bf16[4,256,1024]{2,1,0:T(8,128)(2,1)} %copy.90) | copy-start | bytes 6291460
  390.4 9.6 %all-to-all-start.5 = ((bf16[4,32,1024]{2,1,0:T(8,128)(2,1)}), bf16[4,32,1024]{2,1,0:T(8,128)(2,1)}, u32[]{:S(2)}, u32[]{:S(2)}) async-start(bf16[4,32,1024]{2,1,0:T(8,128)(2,1)} %copy.104), calls=%async_computation.6 | async-start | bytes 524288 | tf_op jit(solution)/shard_map/all_to_all | solution.py:45
  394.5 6.6 %copy-start.11 = (s32[32]{0:T(128)S(1)}, s32[32]{0:T(128)}, u32[]{:S(2)}) copy-start(s32[32]{0:T(128)} %fusion.36) | copy-start | bytes 388
Sparse Core Ops, SparseCore 0:
  9.2 37.1 all-gather.2
  98.8 136.6 reduce-scatter.1
  238.7 80.9 all-gather.4
where the time goes:
time: 412 us; the launch traced here: 410 us
  waiting for transfers between devices  281 us (68%)
  starting transfers between devices  37.4 us (9%)
  local copies, waits for them, and re-layouts  37.1 us (9%)
  other arithmetic  17.5 us (4%)
  between operations  13.6 us (3%)
  matrix products  11.7 us (3%)
  blocking collectives  11.6 us (3%)
    reduce_scatter x1, waiting for transfers between devices, body(): lax.psum_scatter(project(query_rows, source_rows, heavy_input), 'seq', sc...  137 us
    all_gather x1, waiting for transfers between devices, sent_together(): lax.all_gather(both, axis, axis=dim, tiled=True)  73.9 us
    all_gather x1, waiting for transfers between devices, body(): gathered = lax.all_gather(tokens, 'head', axis=1, tiled=True)  31.2 us
    all_to_all x1, waiting for transfers between devices, copy_for_each(): return lax.all_to_all(copies, axis, split_axis=0, concat_axis=0, tiled=True)  12.8 us
    all_gather x1, blocking collectives, body(): every_head = lax.all_gather(light_heads, 'head', axis=1, tiled=True)  11.6 us
    unnamed x35, local copies, waits for them, and re-layouts  10.9 us
    all_to_all x1, starting transfers between devices, body(): lax.all_to_all(pick_rows(gathered, own_sources), 'seq', split_axis=1, con...  10.9 us
    all_to_all x1, waiting for transfers between devices, body(): lax.all_to_all(pick_rows(gathered, own_sources), 'seq', split_axis=1, con...  10.3 us
  transfers between devices with their start and end apart: 9, of which 8 were waited for; matrix products, arithmetic and copies ran while one was open for 9% of the time, Pallas kernels for 0%

commit v1 on v0

v1 whole, which is shorter than its diff:
```python
import functools
import math

import jax
import jax.numpy as jnp
from jax import lax
from jax.experimental import pallas as pl
from jax.experimental.pallas import tpu as pltpu
from jax.sharding import PartitionSpec as P

HD = 128
LB = 128
FB = 128
BF = jnp.bfloat16
F32 = jnp.float32


def dot(a, b):
    return jnp.dot(a, b, preferred_element_type=F32)


def dot_nt(a, b):
    return lax.dot_general(a, b, (((1,), (1,)), ((), ())), preferred_element_type=F32)


def iota(shape, dim):
    return lax.broadcasted_iota(jnp.int32, shape, dim)


def as_column(row):
    n = row.shape[1]
    wide = jnp.broadcast_to(row, (n, n))
    return jnp.sum(jnp.where(iota((n, n), 0) == iota((n, n), 1), wide, 0.0), axis=1, keepdims=True)


def onehot(hit):
    return jnp.where(hit, 1.0, 0.0).astype(BF)


def compact_index(table):
    shards, slots = table.shape
    per = 128 // slots
    rows = shards // per
    spread = onehot(iota((slots, 128), 1) % slots == iota((slots, 128), 0))
    tiled = dot(table.astype(F32).astype(BF), spread)
    keep = iota((shards, 128), 0) % per == iota((shards, 128), 1) // slots
    join = onehot(iota((rows, shards), 1) // per == iota((rows, shards), 0))
    flat = dot(join, jnp.where(keep, tiled, 0.0).astype(BF))
    live = flat >= 0.0
    marks = onehot(live)
    before = dot(marks, onehot(iota((128, 128), 0) < iota((128, 128), 1)))
    in_row = dot(marks, jnp.ones((128, 128), BF))
    above = dot(onehot(iota((rows, rows), 1) < iota((rows, rows), 0)), in_row.astype(BF))
    return jnp.where(live, before + above, -1.0)


def softmax_value(q, k, v):
    scores = dot_nt(q, k) * (1.0 / math.sqrt(HD))
    expanded = jnp.exp(scores - jnp.max(scores, axis=-1, keepdims=True))
    totals = jnp.sum(expanded, axis=-1, keepdims=True)
    return (dot(expanded.astype(BF), v) / totals).astype(BF)


def kernel(
    dims,
    tok, lin, lout, hin, hout, qtab, ctab, gate,
    out,
    picks, landed, comp, sel, xall, wbuf, part, rsum, kv, qbuf, oz, oy,
    wother, wcat, rmine, rother, rsel, ret,
    tall, lw, lo, lmap, lheads, lsend, lrecv, lacc, cidx,
    s1s, s1r, wss, wsr, wos, wor, tks, tkr, xs, xr, rs, rr, kvs, kvr, qs, qr,
    ozs, ozr, oys, oyr, cs, cr, rts, rtr, lrs, lrr, lis, los, self1, self2, self3, self4,
):
    Z, Y, X = dims
    nb = 2 * Y
    S = Z * Y * 2
    R = comp.shape[0]
    rz = R // Z
    slots = qtab.shape[1]
    T = tok.shape[0]
    FX = tok.shape[1]
    s = lax.axis_index("seq")
    x = lax.axis_index("head")
    z = s // (2 * Y)
    y = (s // 2) % Y
    c = s % 2

    def seq_of(zz, yy, cc):
        return (zz * Y + yy) * 2 + cc

    def send(src, dst, ss, rsem, to):
        pltpu.make_async_remote_copy(
            src_ref=src, dst_ref=dst, send_sem=ss, recv_sem=rsem,
            device_id=to, device_id_type=pl.DeviceIdType.MESH,
        ).start()

    def drain(ref, sem):
        pltpu.make_async_copy(ref, ref, sem).wait()

    load_in = pltpu.make_async_copy(lin, lw, lis)
    load_out = pltpu.make_async_copy(lout, lo, los)
    load_in.start()
    load_out.start()

    own_q = qtab[pl.ds(s, 1), :].astype(F32)
    own_c = ctab[pl.ds(s, 1), :].astype(F32)
    for i, row in enumerate((own_q, own_c)):
        want = onehot(as_column(row) == iota((slots, T), 1).astype(F32))
        rows = dot(want, tok[...]).astype(BF)
        for b in range(nb):
            picks[i, b] = rows[:, b * FB:(b + 1) * FB]

    handler = z // 2 == x
    own_block = (z % 2) * Y + y
    fan = nb * X * 2

    def route(i, _):
        n = lax.rem(i + s, fan)
        b = n // (2 * X)
        xt = (n // 2) % X
        ct = n % 2
        st = seq_of(2 * x + b // Y, b % Y, ct)
        here = jnp.logical_and(st == s, xt == x)

        @pl.when(jnp.logical_not(here))
        def _():
            send(picks.at[ct, b], landed.at[s], s1s, s1r, (st, xt))

        return 0

    lax.fori_loop(0, fan, route, 0)

    @pl.when(handler)
    def _():
        landed[pl.ds(s, 1)] = picks[pl.ds(c, 1), pl.ds(own_block, 1)].reshape(1, slots, FB)

    j = 2 * y + c

    def weights_out(i, _):
        jt = lax.rem(j + 1 + i, nb)
        yt = jt // 2
        ct = jt % 2
        cols = pl.ds(pl.multiple_of(yt * 2 * HD, 2 * HD), 2 * HD)

        @pl.when(ct == 0)
        def _():
            send(hin.at[pl.ds(0, 1), :, cols], wbuf.at[pl.ds(0, 1), j], wss, wsr, (seq_of(z, yt, ct), x))

        @pl.when(ct == 1)
        def _():
            send(hin.at[pl.ds(1, 2), :, cols], wbuf.at[pl.ds(0, 2), j], wss, wsr, (seq_of(z, yt, ct), x))

        return 0

    lax.fori_loop(0, nb - 1, weights_out, 0)
    own_cols = pl.ds(pl.multiple_of(y * 2 * HD, 2 * HD), 2 * HD)

    @pl.when(c == 0)
    def _():
        wbuf[pl.ds(0, 1), pl.ds(j, 1)] = hin[pl.ds(0, 1), :, own_cols].reshape(1, 1, hin.shape[1], 2 * HD)

    @pl.when(c == 1)
    def _():
        wbuf[pl.ds(0, 2), pl.ds(j, 1)] = hin[pl.ds(1, 2), :, own_cols].reshape(2, 1, hin.shape[1], 2 * HD)

    twin = (seq_of(z, y, 1 - c), x)
    send(hout.at[:, 1 - c], wother, wos, wor, twin)

    for d in range(1, X):
        send(tok, tall.at[x], tks.at[d], tkr.at[d], (s, lax.rem(x + d, X)))

    q_idx = compact_index(qtab[...])
    c_idx = compact_index(ctab[...])
    mine = jnp.where(c == 0, q_idx, c_idx)
    krows = mine.shape[0]
    row_id = iota((R, 128), 0).astype(F32)
    for k in range(krows):
        comp[:, k * 128:(k + 1) * 128] = onehot(row_id == mine[k:k + 1, :])
    cidx[...] = q_idx
    half = krows // 2
    col_id = iota((128, R), 1).astype(F32)
    for k in range(half):
        column = as_column(cidx[pl.ds(half * c + k, 1), :])
        sel[k * 128:(k + 1) * 128, :] = onehot(column == col_id)

    @pl.when(handler)
    def _():
        drain(landed.at[pl.ds(0, S - 1)], s1r)

    @pl.when(jnp.logical_not(handler))
    def _():
        drain(landed, s1r)

    xall[pl.ds(y, 1)] = dot(comp[...], landed[...].reshape(S * slots, FB)).astype(BF).reshape(1, R, FB)
    for d in range(1, Y):
        send(xall.at[y], xall.at[y], xs, xr, (seq_of(z, lax.rem(y + d, Y), c), x))

    drain(wother, wor)
    place = iota((FB // 2, FB), 1) - iota((FB // 2, FB), 0)
    mine_w = hout[:, pl.ds(c, 1)].reshape(Y * HD, FB // 2)
    their_w = wother[...].reshape(Y * HD, FB // 2)
    wcat[...] = (
        dot(mine_w, onehot(place == (FB // 2) * c)) + dot(their_w, onehot(place == (FB // 2) * (1 - c)))
    ).astype(BF)

    @pl.when(c == 0)
    def _():
        drain(wbuf.at[pl.ds(0, 1), pl.ds(0, nb - 1)], wsr)

    @pl.when(c == 1)
    def _():
        drain(wbuf.at[pl.ds(0, 2), pl.ds(0, nb - 1)], wsr)

    if Y > 1:
        drain(xall.at[pl.ds(0, Y - 1)], xr)

    def projected(i):
        total = None
        for yy in range(Y):
            term = dot(xall[yy], wbuf[i, 2 * yy:2 * yy + 2].reshape(FB, 2 * HD))
            total = term if total is None else total + term
        part[:, i] = total.astype(BF).reshape(Z, rz, 2 * HD)

    projected(0)

    @pl.when(c == 1)
    def _():
        projected(1)

    def sum_out(i, _):
        zt = lax.rem(z + 1 + i, Z)

        @pl.when(c == 0)
        def _():
            send(part.at[zt, pl.ds(0, 1)], rsum.at[z, pl.ds(0, 1)], rs, rr, (seq_of(zt, y, c), x))

        @pl.when(c == 1)
        def _():
            send(part.at[zt], rsum.at[z], rs, rr, (seq_of(zt, y, c), x))

        return 0

    lax.fori_loop(0, Z - 1, sum_out, 0)
    rsum[pl.ds(z, 1), 0:1] = part[pl.ds(z, 1), 0:1]

    @pl.when(c == 1)
    def _():
        rsum[pl.ds(z, 1), 1:2] = part[pl.ds(z, 1), 1:2]

    load_in.wait()

    def project_light(source, at, first):
        def one(i, _):
            term = dot(source[...], lw[i, pl.ds(pl.multiple_of(at * FX, FX), FX), :])
            if first:
                lmap[i] = term
            else:
                lmap[i] += term
            return 0

        lax.fori_loop(0, 3, one, 0)

    project_light(tok, x, True)

    @pl.when(c == 0)
    def _():
        drain(rsum.at[pl.ds(0, Z - 1), pl.ds(0, 1)], rr)
        rows = jnp.sum(rsum[:, 0].astype(F32), axis=0).astype(BF)
        qbuf[0] = rows[:, :HD]
        qbuf[1] = rows[:, HD:]
        send(qbuf.at[1], qbuf.at[0], qs, qr, twin)

    @pl.when(c == 1)
    def _():
        drain(rsum.at[pl.ds(0, Z - 1)], rr)
        for i in range(2):
            rows = jnp.sum(rsum[:, i].astype(F32), axis=0).astype(BF)
            for g in range(2):
                kv[g, i, pl.ds(z, 1)] = rows[:, g * HD:(g + 1) * HD].reshape(1, rz, HD)

        def kv_zero(i, _):
            zt = lax.rem(z + i, Z)
            send(kv.at[0, :, z], kv.at[1, :, z], kvs, kvr, (seq_of(zt, y, 0), x))
            return 0

        def kv_one(i, _):
            zt = lax.rem(z + 1 + i, Z)
            send(kv.at[1, :, z], kv.at[1, :, z], kvs, kvr, (seq_of(zt, y, 1), x))
            return 0

        lax.fori_loop(0, Z, kv_zero, 0)
        lax.fori_loop(0, Z - 1, kv_one, 0)

    for d in range(1, X):
        src = lax.rem(x + X - d, X)
        drain(tall.at[0], tkr.at[d])
        project_light(tall.at[src], src, False)

    @pl.when(c == 0)
    def _():
        drain(kv.at[1], kvr)

    @pl.when(c == 1)
    def _():
        drain(qbuf.at[0], qr)
        drain(kv.at[1, :, pl.ds(0, Z - 1)], kvr)

    heads = softmax_value(qbuf[0], kv[1, 0].reshape(R, HD), kv[1, 1].reshape(R, HD))
    oz[pl.ds(z, 1)] = heads.reshape(1, rz, HD)

    def heads_out(i, _):
        zt = lax.rem(z + 1 + i, Z)
        send(oz.at[z], oz.at[z], ozs, ozr, (seq_of(zt, y, c), x))
        return 0

    lax.fori_loop(0, Z - 1, heads_out, 0)

    for g in range(2):
        for blk in range(T // LB):
            rows = slice(blk * LB, (blk + 1) * LB)
            cols = slice(g * HD, (g + 1) * HD)
            lheads[rows, cols] = softmax_value(
                lmap[0, rows, cols].astype(BF), lmap[1, rows, cols].astype(BF), lmap[2, rows, cols].astype(BF)
            )
    load_out.wait()
    for d in range(1, X):
        xt = lax.rem(x + d, X)
        lsend[pl.ds(xt, 1)] = dot(
            lheads[...], lo[:, pl.ds(pl.multiple_of(xt * FX, FX), FX)]
        ).astype(BF).reshape(1, T, FX)
        send(lsend.at[xt], lrecv.at[x], lrs, lrr, (s, xt))

    drain(oz.at[pl.ds(0, Z - 1)], ozr)
    for d in range(1, Y):
        send(oz, oy.at[y], oys, oyr, (seq_of(z, lax.rem(y + d, Y), c), x))
    oy[pl.ds(y, 1)] = oz[...].reshape(1, Z, rz, HD)
    lacc[...] = dot(lheads[...], lo[:, pl.ds(pl.multiple_of(x * FX, FX), FX)])

    if Y > 1:
        drain(oy.at[pl.ds(0, Y - 1)], oyr)
    total = None
    for yy in range(Y):
        term = dot(oy[yy].reshape(R, HD), wcat[yy * HD:(yy + 1) * HD, :])
        total = term if total is None else total + term
    rmine[...] = total.astype(BF)
    send(rmine, rother, cs, cr, twin)
    drain(rother, cr)
    both = (total + rother[...].astype(F32)).astype(BF)
    rsel[...] = dot(sel[...], both).astype(BF).reshape(S // 2, slots, FB)

    block = pl.ds(pl.multiple_of(own_block * FB, FB), FB)
    xq = z // 2

    def give(i, _):
        n = lax.rem(i + s + x * Y, S // 2)
        st = (S // 2) * c + n
        here = jnp.logical_and(st == s, xq == x)

        @pl.when(jnp.logical_not(here))
        def _():
            send(rsel.at[n], ret.at[x, :, block], rts, rtr, (st, xq))

        return 0

    lax.fori_loop(0, S // 2, give, 0)
    keeps = jnp.logical_and(handler, s // (S // 2) == c)

    @pl.when(keeps)
    def _():
        ret[pl.ds(x, 1), :, block] = rsel[pl.ds(lax.rem(s, S // 2), 1)]

    if X > 1:
        drain(lrecv.at[pl.ds(0, X - 1)], lrr)
    light = lacc[...]
    for d in range(1, X):
        light = light + lrecv[pl.ds(lax.rem(x + d, X), 1)].reshape(T, FX).astype(F32)
    lacc[...] = light
    onto = onehot(own_q == iota((T, slots), 0).astype(F32))
    gates = as_column(gate[...])

    gets = jnp.logical_and(handler, s // (S // 2) == c)

    @pl.when(gets)
    def _():
        drain(landed.at[pl.ds(0, nb * X - 1)], rtr)

    @pl.when(jnp.logical_not(gets))
    def _():
        drain(landed.at[pl.ds(0, nb * X)], rtr)

    update = jnp.sum(ret[...].astype(F32), axis=0) * gates
    high = update.astype(BF)
    low = (update - high.astype(F32)).astype(BF)
    out[...] = (lacc[...] + dot(onto, high) + dot(onto, low)).astype(BF)

    @pl.when(handler)
    def _():
        drain(landed.at[pl.ds(0, fan - 1)], s1s)

    @pl.when(jnp.logical_not(handler))
    def _():
        drain(landed.at[pl.ds(0, fan)], s1s)

    @pl.when(c == 0)
    def _():
        drain(wbuf.at[pl.ds(0, 1), pl.ds(0, Y - 1)], wss) if Y > 1 else None
        drain(wbuf.at[pl.ds(0, 2), pl.ds(0, Y)], wss)

    @pl.when(c == 1)
    def _():
        drain(wbuf.at[pl.ds(0, 1), pl.ds(0, Y)], wss)
        drain(wbuf.at[pl.ds(0, 2), pl.ds(0, Y - 1)], wss) if Y > 1 else None

    drain(wother, wos)
    for d in range(1, X):
        drain(tall.at[0], tks.at[d])
    if Y > 1:
        drain(xall.at[pl.ds(0, Y - 1)], xs)
        drain(oy.at[pl.ds(0, Y - 1)], oys)

    @pl.when(c == 0)
    def _():
        drain(rsum.at[pl.ds(0, Z - 1), pl.ds(0, 1)], rs)
        drain(qbuf.at[0], qs)

    @pl.when(c == 1)
    def _():
        drain(rsum.at[pl.ds(0, Z - 1)], rs)
        drain(kv.at[0], kvs)
        drain(kv.at[0, :, pl.ds(0, Z - 1)], kvs)

    drain(oz.at[pl.ds(0, Z - 1)], ozs)
    drain(rmine, cs)

    @pl.when(keeps)
    def _():
        drain(rsel.at[pl.ds(0, S // 2 - 1)], rts)

    @pl.when(jnp.logical_not(keeps))
    def _():
        drain(rsel, rts)

    if X > 1:
        drain(lrecv.at[pl.ds(0, X - 1)], lrs)


def body(dims, tokens, light_input, light_output, heavy_input, heavy_output, query_tokens, context_tokens, query_gate):
    Z, Y, X = dims
    S = Z * Y * 2
    nb = 2 * Y
    slots = query_tokens.shape[1]
    T, FX = tokens.shape
    R = S * T // 32
    rz = R // Z
    D = light_input.shape[1]
    LX = light_input.shape[2]
    hout = heavy_output.reshape(Y, 2, HD, FB // 2)
    vm = pl.BlockSpec(memory_space=pltpu.VMEM)
    hbm = pl.BlockSpec(memory_space=pl.ANY)
    dma = pltpu.SemaphoreType.DMA
    scratch = [
        pltpu.VMEM((2, nb, slots, FB), BF),
        pltpu.VMEM((S, slots, FB), BF),
        pltpu.VMEM((R, S * slots), BF),
        pltpu.VMEM((S * slots // 2, R), BF),
        pltpu.VMEM((Y, R, FB), BF),
        pltpu.VMEM((2, nb, FB // 2, 2 * HD), BF),
        pltpu.VMEM((Z, 2, rz, 2 * HD), BF),
        pltpu.VMEM((Z, 2, rz, 2 * HD), BF),
        pltpu.VMEM((2, 2, Z, rz, HD), BF),
        pltpu.VMEM((2, rz, HD), BF),
        pltpu.VMEM((Z, rz, HD), BF),
        pltpu.VMEM((Y, Z, rz, HD), BF),
        pltpu.VMEM((Y, HD, FB // 2), BF),
        pltpu.VMEM((Y * HD, FB), BF),
        pltpu.VMEM((R, FB), BF),
        pltpu.VMEM((R, FB), BF),
        pltpu.VMEM((S // 2, slots, FB), BF),
        pltpu.VMEM((X, slots, FX), BF),
        pltpu.VMEM((X, T, FX), BF),
        pltpu.VMEM((3, D, LX), BF),
        pltpu.VMEM((LX, D), BF),
        pltpu.VMEM((3, T, LX), F32),
        pltpu.VMEM((T, LX), BF),
        pltpu.VMEM((X, T, FX), BF),
        pltpu.VMEM((X, T, FX), BF),
        pltpu.VMEM((T, FX), F32),
        pltpu.VMEM((S * slots // 128, 128), F32),
        dma(()), dma(()), dma(()), dma(()), dma(()), dma(()),
        dma((X,)), dma((X,)),
        *[dma(()) for _ in range(24)],
    ]
    return pl.pallas_call(
        functools.partial(kernel, dims),
        out_shape=jax.ShapeDtypeStruct((T, FX), BF),
        in_specs=[vm, hbm, hbm, vm, vm, vm, vm, vm],
        out_specs=vm,
        scratch_shapes=scratch,
        compiler_params=pltpu.CompilerParams(has_side_effects=True, vmem_limit_bytes=56 << 20),
    )(tokens, light_input, light_output, heavy_input, hout, query_tokens, context_tokens, query_gate)


def solution(mesh):
    X = mesh.shape["head"]
    Z = 2 * X
    dims = (Z, mesh.shape["seq"] // (2 * Z), X)
    placed = (
        P("seq", "head"),
        P(None, None, "head"),
        P("head", None),
        P(None, "seq", "head"),
        P("head", "seq"),
        P(),
        P(),
        P("seq", None),
    )
    return jax.shard_map(
        functools.partial(body, dims), mesh=mesh, in_specs=placed, out_specs=P("seq", "head"), check_vma=False
    )
```

time: 412 us -> 126 us (0.31)
  waiting for transfers between devices: 281 us -> 0 us
  Pallas kernels: 0 us -> 118 us
  starting transfers between devices: 37.4 us -> 0 us
  local copies, waits for them, and re-layouts: 37.1 us -> 6.42 us
  other arithmetic: 17.5 us -> 0 us
  between operations: 13.6 us -> 0.01 us
  matrix products: 11.7 us -> 0 us
  blocking collectives: 11.6 us -> 0 us
    reduce_scatter x1 -> x0, waiting for transfers between devices: 137 us -> none  [body(): lax.psum_scatter(project(query_rows, source_rows, heavy_input), 'seq', sc...]
    pallas_call x0 -> x1, Pallas kernels: none -> 118 us  [body(): pl.pallas_call(functools.partial(kernel, dims), out_shape=jax.ShapeDtypeS...]
    all_gather x2 -> x0, waiting for transfers between devices: 105 us -> none  [the longest x1 73.9 us: sent_together(): lax.all_gather(both, axis, axis=dim, tiled=True)]
    all_to_all x6 -> x0, waiting for transfers between devices: 38.2 us -> none  [the longest x1 12.8 us: copy_for_each(): return lax.all_to_all(copies, axis, split_axis=0, concat_axis=0, tiled=True)]
    all_to_all x6 -> x0, starting transfers between devices: 37.3 us -> none  [the longest x1 10.9 us: body(): lax.all_to_all(pick_rows(gathered, own_sources), 'seq', split_axis=1, con...]
    gather x7 -> x0, local copies, waits for them, and re-layouts: 12.6 us -> none  [the longest x1 6.18 us: body(): jnp.take(heavy_part, jnp.where(slot_live, compact, 0).reshape(-1), axis=0)]
    dot_general x8 -> x0, matrix products: 11.7 us -> none  [the longest x1 4.61 us: body(): jnp.einsum('td,cdw->ctw', gathered, light_input, preferred_element_type=j...]
    all_gather x1 -> x0, blocking collectives: 11.6 us -> none  [body(): every_head = lax.all_gather(light_heads, 'head', axis=1, tiled=True)]
  transfers between devices with their start and end apart: 9 -> 0, of which waited for: 8 -> 0; matrix products, arithmetic and copies ran while one was open for 9% -> 0% of each run, Pallas kernels for 0% -> 0%
where the time goes in v1:
time: 126 us; the launch traced here: 125 us
  Pallas kernels  118 us (94%)
  local copies, waits for them, and re-layouts  6.42 us (5%)
    pallas_call x1, Pallas kernels, body(): pl.pallas_call(functools.partial(kernel, dims), out_shape=jax.ShapeDtypeS...  118 us
    unnamed x4, local copies, waits for them, and re-layouts  6.42 us

profile of v1, /device:TPU:1, one launch (start us, length us, event | category | flops | bytes accessed | tf_op | source)
XLA Modules:
  0.0 124.9 jit_solution(12716437908802363605)
XLA Ops:
  0.0 1.4 %copy.10.qtab = s32[64,32]{1,0:T(8,128)} copy(s32[64,32]{0,1:T(8,128)} %param.13) | data formatting | bytes 16384 | tf_op args[5]
  1.4 1.4 %copy.11.ctab = s32[64,32]{1,0:T(8,128)} copy(s32[64,32]{0,1:T(8,128)} %param.14) | data formatting | bytes 16384 | tf_op args[6]
  2.8 1.7 %copy.9 = bf16[1024,64]{1,0:T(8,128)(2,1)} copy(bf16[1024,64]{0,1:T(8,128)(2,1)} %param.12) | data formatting | bytes 262144 | tf_op args[4]
  4.6 118.5 %shard_map.82 = bf16[256,1024]{1,0:T(8,128)(2,1)} custom-call(bf16[256,1024]{1,0:T(8,128)(2,1)} %tok.1, bf16[3,4096,256]{2,1,0:T(8,128)(2,1)} %lin.1, bf16[256,4096]{1,0:T(8,128)(2,1)} %lout.1, bf16[3,64,1024]{2,1,0:T(8,128)(2,1)} %hin.1, bf16[4,2,128,64]{3,2,1,0:T(8,128)(2,1)} %bitcast.1, s32[64,32]{1,0:T(8,128)} %copy.10.qtab, s32[64,32]{1,0:T(8,128)} %copy.11.ctab, ...), custom_call_target="tpu_custom_call" | custom-call | tf_op jit(solution)/shard_map/pallas_call | solution.py:493
  123.0 1.9 %copy.13 = bf16[256,1024]{1,0:T(8,128)(2,1)} copy(bf16[256,1024]{1,0:T(8,128)(2,1)} %shard_map.82) | data formatting | bytes 1048576

commit v2 on v1

v2 whole, which is shorter than its diff:
```python
import functools
import math

import jax
import jax.numpy as jnp
from jax import lax
from jax.experimental import pallas as pl
from jax.experimental.pallas import tpu as pltpu
from jax.sharding import PartitionSpec as P

HD = 128
LB = 128
FB = 128
BF = jnp.bfloat16
F32 = jnp.float32


def dot(a, b):
    return jnp.dot(a, b, preferred_element_type=F32)


def dot_nt(a, b):
    return lax.dot_general(a, b, (((1,), (1,)), ((), ())), preferred_element_type=F32)


def iota(shape, dim):
    return lax.broadcasted_iota(jnp.int32, shape, dim)


def as_column(row):
    n = row.shape[1]
    wide = jnp.broadcast_to(row, (n, n))
    return jnp.sum(jnp.where(iota((n, n), 0) == iota((n, n), 1), wide, 0.0), axis=1, keepdims=True)


def as_row(column):
    n = column.shape[0]
    wide = jnp.broadcast_to(column, (n, n))
    return jnp.sum(jnp.where(iota((n, n), 0) == iota((n, n), 1), wide, 0.0), axis=0, keepdims=True)


def onehot(hit):
    return jnp.where(hit, 1.0, 0.0).astype(BF)


def compact_index(table):
    slots, shards = table.shape
    per = 128 // slots
    rows = shards // per
    spread = onehot(iota((128, slots), 0) % slots == iota((128, slots), 1))
    tiled = dot(spread, table.astype(F32).astype(BF))
    keep = iota((128, shards), 1) % per == iota((128, shards), 0) // slots
    join = onehot(iota((rows, shards), 1) // per == iota((rows, shards), 0))
    flat = dot_nt(join, jnp.where(keep, tiled, 0.0).astype(BF))
    live = flat >= 0.0
    marks = onehot(live)
    before = dot(marks, onehot(iota((128, 128), 0) < iota((128, 128), 1)))
    in_row = dot(marks, jnp.ones((128, 128), BF))
    above = dot(onehot(iota((rows, rows), 1) < iota((rows, rows), 0)), in_row.astype(BF))
    return jnp.where(live, before + above, -1.0)


def softmax_value(q, k, v):
    scores = dot_nt(q, k) * (1.0 / math.sqrt(HD))
    expanded = jnp.exp(scores - jnp.max(scores, axis=-1, keepdims=True))
    totals = jnp.sum(expanded, axis=-1, keepdims=True)
    return (dot(expanded.astype(BF), v) / totals).astype(BF)


def kernel(
    dims,
    tok_any, lin, lout, hin_any, hout_any, qtab_any, ctab_any, gate_any,
    out,
    tok, hin, hout, qtab, ctab, gate,
    picks, planes, landed, comp, sel, xall, wbuf, part, rsum, kv, qbuf, oz, oy,
    wcat, rmine, rother, rsel, ret,
    tall, lw, lo, lmap, lheads, lsend, lfar, lrecv, lacc, cidx,
    s0s, s0r, s1s, s1r, wss, wsr, wos, wor, rs, rr, kvs, kvr, qs, qr,
    ozs, ozr, oys, oyr, cs, cr, rts, rtr, lrs, lrr, lis, los,
    tks, tkr, xs, xr, lfr, ins,
):
    Z, Y, X = dims
    NY = Y // X
    nb = 2 * Y
    S = Z * Y * 2
    R = comp.shape[0]
    rz = R // Z
    slots = qtab.shape[0]
    T = tok.shape[0]
    FX = tok.shape[1]
    s = lax.axis_index("seq")
    x = lax.axis_index("head")
    z = s // (2 * Y)
    y = (s // 2) % Y
    c = s % 2
    right, left = lax.rem(x + 1, X), lax.rem(x + X - 1, X)
    far = lax.rem(x + 2, X)

    def seq_of(zz, yy, cc):
        return (zz * Y + yy) * 2 + cc

    twin = (seq_of(z, y, 1 - c), x)

    def send(src, dst, ss, rsem, to):
        pltpu.make_async_remote_copy(
            src_ref=src, dst_ref=dst, send_sem=ss, recv_sem=rsem,
            device_id=to, device_id_type=pl.DeviceIdType.MESH,
        ).start()

    def drain(ref, sem):
        pltpu.make_async_copy(ref, ref, sem).wait()

    barrier = pltpu.get_barrier_semaphore()

    def greet(to):
        pl.semaphore_signal(barrier, inc=1, device_id=to, device_id_type=pl.DeviceIdType.MESH)

    handler = y % X == x

    for d in range(1, nb):
        jt = lax.rem(2 * y + c + d, nb)
        greet((seq_of(z, jt // 2, jt % 2), x))
    for d in range(1, X):
        greet((s, lax.rem(x + d, X)))

    @pl.when(handler)
    def _():
        def greet_plane(i, _):
            greet((lax.rem(s + 1 + i, S), x))
            return 0

        lax.fori_loop(0, S - 1, greet_plane, 0)

    fetches = [
        pltpu.make_async_copy(src, dst, ins.at[i])
        for i, (src, dst) in enumerate((
            (qtab_any, qtab), (ctab_any, ctab), (tok_any, tok), (hin_any, hin), (hout_any, hout), (gate_any, gate),
        ))
    ]
    for fetch in fetches:
        fetch.start()
    load_in = pltpu.make_async_copy(lin, lw, lis)
    load_out = pltpu.make_async_copy(lout, lo, los)
    load_in.start()
    load_out.start()

    fetches[0].wait()
    fetches[1].wait()
    here_s = iota((slots, S), 1) == s
    own_q = jnp.sum(jnp.where(here_s, qtab[...].astype(F32), 0.0), axis=1, keepdims=True)
    own_c = jnp.sum(jnp.where(here_s, ctab[...].astype(F32), 0.0), axis=1, keepdims=True)
    fetches[2].wait()
    for i, column in enumerate((own_q, own_c)):
        want = onehot(column == iota((slots, T), 1).astype(F32))
        rows = dot(want, tok[...]).astype(BF)
        for b in range(nb):
            picks[b % Y, b // Y, i] = rows[:, b * FB:(b + 1) * FB]

    met = (nb - 1) + (X - 1) + NY * Z * 2

    @pl.when(handler)
    def _():
        pl.semaphore_wait(barrier, met - 1)

    @pl.when(jnp.logical_not(handler))
    def _():
        pl.semaphore_wait(barrier, met)

    for d in range(1, X):
        xt = lax.rem(x + d, X)
        for i in range(NY):
            send(picks.at[i * X + xt], planes.at[i, x], s0s, s0r, (s, xt))
    for i in range(NY):
        planes[i, pl.ds(x, 1)] = picks[pl.ds(i * X + x, 1)]

    mine_rows = pl.ds(pl.multiple_of(c * (FB // 2), FB // 2), FB // 2)
    fetches[3].wait()
    fetches[4].wait()
    fetches[5].wait()
    for yy in range(Y):
        wcat[mine_rows, yy * HD:(yy + 1) * HD] = hout[:, pl.ds(pl.multiple_of((2 * yy + c) * HD, HD), HD)]
    if X > 1:
        drain(planes.at[:, pl.ds(0, X - 1)], s0r)

    fan = NY * Z * 2

    def route(i, _):
        n = lax.rem(i + 2 * z + c, fan)
        yi = n // (2 * Z)
        zt = (n // 2) % Z
        ct = n % 2
        st = seq_of(zt, yi * X + x, ct)

        @pl.when(st != s)
        def _():
            send(planes.at[yi, zt // 2, zt % 2, ct], landed.at[s], s1s, s1r, (st, x))

        return 0

    lax.fori_loop(0, fan, route, 0)

    @pl.when(handler)
    def _():
        landed[pl.ds(s, 1)] = planes[
            pl.ds(y // X, 1), pl.ds(z // 2, 1), pl.ds(z % 2, 1), pl.ds(c, 1)
        ].reshape(1, slots, FB)

    j = 2 * y + c

    def weights_out(i, _):
        jt = lax.rem(j + 1 + i, nb)
        yt = jt // 2
        ct = jt % 2
        cols = pl.ds(pl.multiple_of(yt * 2 * HD, 2 * HD), 2 * HD)

        @pl.when(ct == 0)
        def _():
            send(hin.at[pl.ds(0, 1), :, cols], wbuf.at[pl.ds(0, 1), j], wss, wsr, (seq_of(z, yt, ct), x))

        @pl.when(ct == 1)
        def _():
            send(hin.at[pl.ds(1, 2), :, cols], wbuf.at[pl.ds(0, 2), j], wss, wsr, (seq_of(z, yt, ct), x))

        return 0

    lax.fori_loop(0, nb - 1, weights_out, 0)
    own_cols = pl.ds(pl.multiple_of(y * 2 * HD, 2 * HD), 2 * HD)

    @pl.when(c == 0)
    def _():
        wbuf[pl.ds(0, 1), pl.ds(j, 1)] = hin[pl.ds(0, 1), :, own_cols].reshape(1, 1, hin.shape[1], 2 * HD)

    @pl.when(c == 1)
    def _():
        wbuf[pl.ds(0, 2), pl.ds(j, 1)] = hin[pl.ds(1, 2), :, own_cols].reshape(2, 1, hin.shape[1], 2 * HD)

    for yy in range(Y):
        theirs = pl.ds(pl.multiple_of((2 * yy + 1 - c) * HD, HD), HD)
        send(hout.at[:, theirs], wcat.at[mine_rows, pl.ds(yy * HD, HD)], wos, wor, twin)

    q_idx = compact_index(qtab[...])
    c_idx = compact_index(ctab[...])
    krows = q_idx.shape[0]

    @pl.when(handler)
    def _():
        mine = jnp.where(c == 0, q_idx, c_idx)
        row_id = iota((R, 128), 0).astype(F32)
        for k in range(krows):
            comp[:, k * 128:(k + 1) * 128] = onehot(row_id == mine[k:k + 1, :])

    rh = R // 2
    lower, upper = pl.ds(0, rh), pl.ds(rh, rh)

    @pl.when(handler)
    def _():
        drain(landed.at[pl.ds(0, S - 1)], s1r)
        xall[pl.ds(y, 1)] = dot(comp[...], landed[...].reshape(S * slots, FB)).astype(BF).reshape(1, R, FB)
        for d in range(1, X):
            send(xall.at[y, lower], xall.at[y, lower], xs.at[0], xr.at[0], (s, lax.rem(x + d, X)))
        for d in range(1, Y):
            send(xall.at[y, upper], xall.at[y, upper], xs.at[1], xr.at[1], (seq_of(z, lax.rem(y + d, Y), c), x))

    cidx[...] = q_idx
    half = krows // 2
    col_id = iota((128, R), 1).astype(F32)
    for k in range(half):
        column = as_column(cidx[pl.ds(half * c + k, 1), :])
        sel[k * 128:(k + 1) * 128, :] = onehot(column == col_id)

    @pl.when(jnp.logical_not(handler))
    def _():
        drain(xall.at[0, lower], xr.at[0])

    for d in range(1, Y):
        send(xall.at[y, lower], xall.at[y, lower], xs.at[2], xr.at[2], (seq_of(z, lax.rem(y + d, Y), c), x))

    @pl.when(jnp.logical_not(handler))
    def _():
        drain(xall.at[pl.ds(0, NY), lower], xr.at[1])

    if NY > 1:
        @pl.when(handler)
        def _():
            drain(xall.at[pl.ds(0, NY - 1), lower], xr.at[1])

    for d in range(1, X):
        for i in range(NY):
            u = i * X + x
            send(xall.at[u, upper], xall.at[u, upper], xs.at[3], xr.at[3], (s, lax.rem(x + d, X)))

    if X > 1:
        send(tok, tall.at[x], tks.at[0], tkr.at[0], (s, right))
    if X > 2:
        send(tok, tall.at[x], tks.at[1], tkr.at[1], (s, left))

    @pl.when(c == 0)
    def _():
        drain(wbuf.at[pl.ds(0, 1), pl.ds(0, nb - 1)], wsr)

    @pl.when(c == 1)
    def _():
        drain(wbuf.at[pl.ds(0, 2), pl.ds(0, nb - 1)], wsr)

    if Y > 1:
        drain(xall.at[pl.ds(0, Y - 1), lower], xr.at[2])
    if X > 1:
        drain(xall.at[pl.ds(0, NY * (X - 1)), upper], xr.at[3])

    def projected(i):
        total = None
        for yy in range(Y):
            term = dot(xall[yy], wbuf[i, 2 * yy:2 * yy + 2].reshape(FB, 2 * HD))
            total = term if total is None else total + term
        part[:, i] = total.astype(BF).reshape(Z, rz, 2 * HD)

    projected(0)

    @pl.when(c == 1)
    def _():
        projected(1)

    def sum_out(i, _):
        zt = lax.rem(z + 1 + i, Z)

        @pl.when(c == 0)
        def _():
            send(part.at[zt, pl.ds(0, 1)], rsum.at[z, pl.ds(0, 1)], rs, rr, (seq_of(zt, y, c), x))

        @pl.when(c == 1)
        def _():
            send(part.at[zt], rsum.at[z], rs, rr, (seq_of(zt, y, c), x))

        return 0

    lax.fori_loop(0, Z - 1, sum_out, 0)
    rsum[pl.ds(z, 1), 0:1] = part[pl.ds(z, 1), 0:1]

    @pl.when(c == 1)
    def _():
        rsum[pl.ds(z, 1), 1:2] = part[pl.ds(z, 1), 1:2]

    load_in.wait()

    def project_light(source, at, first):
        def one(i, _):
            term = dot(source[...], lw[i, pl.ds(pl.multiple_of(at * FX, FX), FX), :])
            if first:
                lmap[i] = term
            else:
                lmap[i] += term
            return 0

        lax.fori_loop(0, 3, one, 0)

    project_light(tok, x, True)

    th = T // 2
    front, back = pl.ds(0, th), pl.ds(th, th)
    if X > 1:
        drain(tall.at[0], tkr.at[0])
    if X > 2:
        send(tall.at[left, front], tall.at[left, front], tks.at[2], tkr.at[2], (s, right))
        drain(tall.at[0], tkr.at[1])
        send(tall.at[right, back], tall.at[right, back], tks.at[3], tkr.at[3], (s, left))

    @pl.when(c == 0)
    def _():
        drain(rsum.at[pl.ds(0, Z - 1), pl.ds(0, 1)], rr)
        rows = jnp.sum(rsum[:, 0].astype(F32), axis=0).astype(BF)
        qbuf[0] = rows[:, :HD]
        qbuf[1] = rows[:, HD:]
        send(qbuf.at[1], qbuf.at[0], qs, qr, twin)

    @pl.when(c == 1)
    def _():
        drain(rsum.at[pl.ds(0, Z - 1)], rr)
        for i in range(2):
            rows = jnp.sum(rsum[:, i].astype(F32), axis=0).astype(BF)
            for g in range(2):
                kv[g, i, pl.ds(z, 1)] = rows[:, g * HD:(g + 1) * HD].reshape(1, rz, HD)

        def kv_zero(i, _):
            zt = lax.rem(z + i, Z)
            send(kv.at[0, :, z], kv.at[1, :, z], kvs, kvr, (seq_of(zt, y, 0), x))
            return 0

        def kv_one(i, _):
            zt = lax.rem(z + 1 + i, Z)
            send(kv.at[1, :, z], kv.at[1, :, z], kvs, kvr, (seq_of(zt, y, 1), x))
            return 0

        lax.fori_loop(0, Z, kv_zero, 0)
        lax.fori_loop(0, Z - 1, kv_one, 0)

    if X > 1:
        project_light(tall.at[left], left, False)
    if X > 2:
        project_light(tall.at[right], right, False)
        drain(tall.at[0, front], tkr.at[2])
        drain(tall.at[0, back], tkr.at[3])
        project_light(tall.at[far], far, False)

    for g in range(2):
        for blk in range(T // LB):
            rows = slice(blk * LB, (blk + 1) * LB)
            cols = slice(g * HD, (g + 1) * HD)
            lheads[rows, cols] = softmax_value(
                lmap[0, rows, cols].astype(BF), lmap[1, rows, cols].astype(BF), lmap[2, rows, cols].astype(BF)
            )
    load_out.wait()

    def light_out(xt):
        return dot(lheads[...], lo[:, pl.ds(pl.multiple_of(xt * FX, FX), FX)])

    if X > 2:
        lsend[2] = light_out(far).astype(BF)
        send(lsend.at[2, front], lfar.at[0], lrs, lfr.at[0], (s, right))
        send(lsend.at[2, back], lfar.at[1], lrs, lfr.at[1], (s, left))
    if X > 1:
        lsend[0] = light_out(right).astype(BF)
    if X > 2:
        send(lsend.at[0, back], lrecv.at[0, back], lrs, lrr, (s, right))
        lsend[1] = light_out(left).astype(BF)
        send(lsend.at[1, front], lrecv.at[1, front], lrs, lrr, (s, left))
    elif X > 1:
        send(lsend.at[0], lrecv.at[0], lrs, lrr, (s, right))

    @pl.when(c == 0)
    def _():
        drain(kv.at[1], kvr)

    @pl.when(c == 1)
    def _():
        drain(qbuf.at[0], qr)
        drain(kv.at[1, :, pl.ds(0, Z - 1)], kvr)

    heads = softmax_value(qbuf[0], kv[1, 0].reshape(R, HD), kv[1, 1].reshape(R, HD))
    oz[pl.ds(z, 1)] = heads.reshape(1, rz, HD)

    def heads_out(i, _):
        zt = lax.rem(z + 1 + i, Z)
        send(oz.at[z], oz.at[z], ozs, ozr, (seq_of(zt, y, c), x))
        return 0

    lax.fori_loop(0, Z - 1, heads_out, 0)
    lacc[...] = light_out(x)

    if X > 2:
        drain(lfar.at[0], lfr.at[0])
        lsend[0, :th] = (lsend[0, :th].astype(F32) + lfar[0].astype(F32)).astype(BF)
        send(lsend.at[0, front], lrecv.at[0, front], lrs, lrr, (s, right))
        drain(lfar.at[1], lfr.at[1])
        lsend[1, th:] = (lsend[1, th:].astype(F32) + lfar[1].astype(F32)).astype(BF)
        send(lsend.at[1, back], lrecv.at[1, back], lrs, lrr, (s, left))

    drain(oz.at[pl.ds(0, Z - 1)], ozr)
    for d in range(1, Y):
        send(oz, oy.at[y], oys, oyr, (seq_of(z, lax.rem(y + d, Y), c), x))
    oy[pl.ds(y, 1)] = oz[...].reshape(1, Z, rz, HD)
    drain(wcat.at[pl.ds(0, FB // 2)], wor)
    if Y > 1:
        drain(oy.at[pl.ds(0, Y - 1)], oyr)
    total = None
    for yy in range(Y):
        term = dot_nt(oy[yy].reshape(R, HD), wcat[:, yy * HD:(yy + 1) * HD])
        total = term if total is None else total + term
    rmine[...] = total.astype(BF)
    send(rmine, rother, cs, cr, twin)
    drain(rother, cr)
    both = (total + rother[...].astype(F32)).astype(BF)
    rsel[...] = dot(sel[...], both).astype(BF).reshape(S // 2, slots, FB)

    block = pl.ds(pl.multiple_of(((z % 2) * Y + y) * FB, FB), FB)
    xq = z // 2

    def give(i, _):
        n = lax.rem(i + s + x * Y, S // 2)
        st = (S // 2) * c + n
        here = jnp.logical_and(st == s, xq == x)

        @pl.when(jnp.logical_not(here))
        def _():
            send(rsel.at[n], ret.at[x, :, block], rts, rtr, (st, xq))

        return 0

    lax.fori_loop(0, S // 2, give, 0)
    keeps = jnp.logical_and(xq == x, s // (S // 2) == c)

    @pl.when(keeps)
    def _():
        ret[pl.ds(x, 1), :, block] = rsel[pl.ds(lax.rem(s, S // 2), 1)]

    if X > 2:
        drain(lrecv, lrr)
        lacc[...] = lacc[...] + lrecv[0].astype(F32) + lrecv[1].astype(F32)
    elif X > 1:
        drain(lrecv.at[0], lrr)
        lacc[...] = lacc[...] + lrecv[0].astype(F32)
    onto = onehot(as_row(own_q) == iota((T, slots), 0).astype(F32))
    gates = as_column(gate[...])

    @pl.when(keeps)
    def _():
        drain(landed.at[pl.ds(0, nb * X - 1)], rtr)

    @pl.when(jnp.logical_not(keeps))
    def _():
        drain(landed.at[pl.ds(0, nb * X)], rtr)

    update = jnp.sum(ret[...].astype(F32), axis=0) * gates
    high = update.astype(BF)
    low = (update - high.astype(F32)).astype(BF)
    out[...] = (lacc[...] + dot(onto, high) + dot(onto, low)).astype(BF)

    if X > 1:
        drain(planes.at[:, pl.ds(0, X - 1)], s0s)
        drain(xall.at[pl.ds(0, NY * (X - 1)), upper], xs.at[3])
        drain(tall.at[0], tks.at[0])

    @pl.when(handler)
    def _():
        drain(landed.at[pl.ds(0, fan - 1)], s1s)
        if X > 1:
            drain(xall.at[pl.ds(0, X - 1), lower], xs.at[0])
        if Y > 1:
            drain(xall.at[pl.ds(0, Y - 1), upper], xs.at[1])

    @pl.when(jnp.logical_not(handler))
    def _():
        drain(landed.at[pl.ds(0, fan)], s1s)

    @pl.when(c == 0)
    def _():
        if Y > 1:
            drain(wbuf.at[pl.ds(0, 1), pl.ds(0, Y - 1)], wss)
        drain(wbuf.at[pl.ds(0, 2), pl.ds(0, Y)], wss)

    @pl.when(c == 1)
    def _():
        drain(wbuf.at[pl.ds(0, 1), pl.ds(0, Y)], wss)
        if Y > 1:
            drain(wbuf.at[pl.ds(0, 2), pl.ds(0, Y - 1)], wss)

    drain(wcat.at[pl.ds(0, FB // 2)], wos)
    if X > 2:
        drain(tall.at[0], tks.at[1])
        drain(tall.at[0, front], tks.at[2])
        drain(tall.at[0, back], tks.at[3])
        drain(lsend, lrs)
    elif X > 1:
        drain(lsend.at[0], lrs)
    if Y > 1:
        drain(xall.at[pl.ds(0, Y - 1), lower], xs.at[2])
        drain(oy.at[pl.ds(0, Y - 1)], oys)

    @pl.when(c == 0)
    def _():
        drain(rsum.at[pl.ds(0, Z - 1), pl.ds(0, 1)], rs)
        drain(qbuf.at[0], qs)

    @pl.when(c == 1)
    def _():
        drain(rsum.at[pl.ds(0, Z - 1)], rs)
        drain(kv.at[0], kvs)
        drain(kv.at[0, :, pl.ds(0, Z - 1)], kvs)

    drain(oz.at[pl.ds(0, Z - 1)], ozs)
    drain(rmine, cs)

    @pl.when(keeps)
    def _():
        drain(rsel.at[pl.ds(0, S // 2 - 1)], rts)

    @pl.when(jnp.logical_not(keeps))
    def _():
        drain(rsel, rts)


def body(dims, tokens, light_input, light_output, heavy_input, heavy_output, query_tokens, context_tokens, query_gate):
    Z, Y, X = dims
    S = Z * Y * 2
    nb = 2 * Y
    slots = query_tokens.shape[1]
    T, FX = tokens.shape
    R = S * T // 32
    rz = R // Z
    D = light_input.shape[1]
    LX = light_input.shape[2]
    hbm = pl.BlockSpec(memory_space=pl.ANY)
    dma = pltpu.SemaphoreType.DMA
    scratch = [
        pltpu.VMEM((T, FX), BF),
        pltpu.VMEM(heavy_input.shape, BF),
        pltpu.VMEM((FB // 2, 2 * Y * HD), BF),
        pltpu.VMEM((slots, S), jnp.int32),
        pltpu.VMEM((slots, S), jnp.int32),
        pltpu.VMEM((1, slots), F32),
        pltpu.VMEM((Y, 2, 2, slots, FB), BF),
        pltpu.VMEM((Y // X, X, 2, 2, slots, FB), BF),
        pltpu.VMEM((S, slots, FB), BF),
        pltpu.VMEM((R, S * slots), BF),
        pltpu.VMEM((S * slots // 2, R), BF),
        pltpu.VMEM((Y, R, FB), BF),
        pltpu.VMEM((2, nb, FB // 2, 2 * HD), BF),
        pltpu.VMEM((Z, 2, rz, 2 * HD), BF),
        pltpu.VMEM((Z, 2, rz, 2 * HD), BF),
        pltpu.VMEM((2, 2, Z, rz, HD), BF),
        pltpu.VMEM((2, rz, HD), BF),
        pltpu.VMEM((Z, rz, HD), BF),
        pltpu.VMEM((Y, Z, rz, HD), BF),
        pltpu.VMEM((FB, Y * HD), BF),
        pltpu.VMEM((R, FB), BF),
        pltpu.VMEM((R, FB), BF),
        pltpu.VMEM((S // 2, slots, FB), BF),
        pltpu.VMEM((X, slots, FX), BF),
        pltpu.VMEM((X, T, FX), BF),
        pltpu.VMEM((3, D, LX), BF),
        pltpu.VMEM((LX, D), BF),
        pltpu.VMEM((3, T, LX), F32),
        pltpu.VMEM((T, LX), BF),
        pltpu.VMEM((3, T, FX), BF),
        pltpu.VMEM((2, T // 2, FX), BF),
        pltpu.VMEM((2, T, FX), BF),
        pltpu.VMEM((T, FX), F32),
        pltpu.VMEM((S * slots // 128, 128), F32),
        *[dma(()) for _ in range(26)],
        dma((4,)), dma((4,)), dma((4,)), dma((4,)), dma((2,)), dma((6,)),
    ]
    return pl.pallas_call(
        functools.partial(kernel, dims),
        out_shape=jax.ShapeDtypeStruct((T, FX), BF),
        in_specs=[hbm] * 8,
        out_specs=pl.BlockSpec(memory_space=pltpu.VMEM),
        scratch_shapes=scratch,
        compiler_params=pltpu.CompilerParams(collective_id=0, has_side_effects=True, vmem_limit_bytes=56 << 20),
    )(
        tokens, light_input, light_output, heavy_input, heavy_output.T, query_tokens.T, context_tokens.T, query_gate
    )


def solution(mesh):
    X = mesh.shape["head"]
    Z = 2 * X
    dims = (Z, mesh.shape["seq"] // (2 * Z), X)
    placed = (
        P("seq", "head"),
        P(None, None, "head"),
        P("head", None),
        P(None, "seq", "head"),
        P("head", "seq"),
        P(),
        P(),
        P("seq", None),
    )
    return jax.shard_map(
        functools.partial(body, dims), mesh=mesh, in_specs=placed, out_specs=P("seq", "head"), check_vma=False
    )
```

time: 126 us -> 84.6 us (0.67)
  the two profiles are of different devices: /device:TPU:1 before, /device:TPU:37 now
where the time goes in v2:
time: 84.6 us; the launch traced here: 84.4 us
  Pallas kernels  82.5 us (98%)
  local copies, waits for them, and re-layouts  1.87 us (2%)
    pallas_call x1, Pallas kernels, body(): pl.pallas_call(functools.partial(kernel, dims), out_shape=jax.ShapeDtypeS...  82.5 us
    unnamed x1, local copies, waits for them, and re-layouts  1.87 us

profile of v2, /device:TPU:37, one launch (start us, length us, event | category | flops | bytes accessed | tf_op | source)
XLA Modules:
  0.0 84.4 jit_solution(6339614722277750337)
XLA Ops:
  0.0 82.5 %shard_map.82 = bf16[256,1024]{1,0:T(8,128)(2,1)} custom-call(bf16[256,1024]{1,0:T(8,128)(2,1)} %tok_any.1, bf16[3,4096,256]{2,1,0:T(8,128)(2,1)} %lin.1, bf16[256,4096]{1,0:T(8,128)(2,1)} %lout.1, bf16[3,64,1024]{2,1,0:T(8,128)(2,1)} %hin_any.1, bf16[64,1024]{1,0:T(8,128)(2,1)} %bitcast.3, s32[32,64]{1,0:T(8,128)} %bitcast.4, s32[32,64]{1,0:T(8,128)} %bitcast.5, ...), custom_call_target="tpu_custom_call" | custom-call | tf_op jit(solution)/shard_map/pallas_call | solution.py:631
  82.5 1.9 %copy.10 = bf16[256,1024]{1,0:T(8,128)(2,1)} copy(bf16[256,1024]{1,0:T(8,128)(2,1)} %shard_map.82) | data formatting | bytes 1048576

commit v3 on v2

--- a/solution.py
+++ b/solution.py
@@ -100,6 +100,7 @@
         return (zz * Y + yy) * 2 + cc
 
     twin = (seq_of(z, y, 1 - c), x)
+    others = sorted(range(1, Z), key=lambda d: -min(d, Z - d))
 
     def send(src, dst, ss, rsem, to):
         pltpu.make_async_remote_copy(
@@ -115,7 +116,8 @@
     def greet(to):
         pl.semaphore_signal(barrier, inc=1, device_id=to, device_id_type=pl.DeviceIdType.MESH)
 
-    handler = y % X == x
+    unit = (y + c * (Y // 2)) % Y
+    handler = unit % X == x
 
     for d in range(1, nb):
         jt = lax.rem(2 * y + c + d, nb)
@@ -189,7 +191,7 @@
         yi = n // (2 * Z)
         zt = (n // 2) % Z
         ct = n % 2
-        st = seq_of(zt, yi * X + x, ct)
+        st = seq_of(zt, (yi * X + x + Y - ct * (Y // 2)) % Y, ct)
 
         @pl.when(st != s)
         def _():
@@ -202,8 +204,16 @@
     @pl.when(handler)
     def _():
         landed[pl.ds(s, 1)] = planes[
-            pl.ds(y // X, 1), pl.ds(z // 2, 1), pl.ds(z % 2, 1), pl.ds(c, 1)
+            pl.ds(unit // X, 1), pl.ds(z // 2, 1), pl.ds(z % 2, 1), pl.ds(c, 1)
         ].reshape(1, slots, FB)
+
+    th = T // 2
+    front, back = pl.ds(0, th), pl.ds(th, th)
+    if X > 2:
+        send(tok.at[front], tall.at[x, front], tks.at[0], tkr.at[0], (s, right))
+        send(tok.at[back], tall.at[x, back], tks.at[1], tkr.at[1], (s, left))
+    elif X > 1:
+        send(tok, tall.at[x], tks.at[0], tkr.at[0], (s, right))
 
     j = 2 * y + c
 
@@ -255,17 +265,31 @@
     @pl.when(handler)
     def _():
         drain(landed.at[pl.ds(0, S - 1)], s1r)
-        xall[pl.ds(y, 1)] = dot(comp[...], landed[...].reshape(S * slots, FB)).astype(BF).reshape(1, R, FB)
-        for d in range(1, X):
-            send(xall.at[y, lower], xall.at[y, lower], xs.at[0], xr.at[0], (s, lax.rem(x + d, X)))
-        for d in range(1, Y):
-            send(xall.at[y, upper], xall.at[y, upper], xs.at[1], xr.at[1], (seq_of(z, lax.rem(y + d, Y), c), x))
+        for part_rows in (lower, upper):
+            xall[pl.ds(unit, 1), part_rows] = dot(
+                comp[part_rows, :], landed[...].reshape(S * slots, FB)
+            ).astype(BF).reshape(1, rh, FB)
+            if part_rows is lower:
+                for d in range(1, X):
+                    send(xall.at[unit, lower], xall.at[unit, lower], xs.at[0], xr.at[0], (s, lax.rem(x + d, X)))
+            else:
+                for d in range(1, Y):
+                    send(
+                        xall.at[unit, upper], xall.at[unit, upper], xs.at[1], xr.at[1],
+                        (seq_of(z, lax.rem(y + d, Y), c), x),
+                    )
 
     cidx[...] = q_idx
     half = krows // 2
+    per_z = krows // Z
+
+    def back_row(k):
+        ahead = jnp.where(c == 0, Z // 2 - 1 - k // per_z, Z // 2 + k // per_z)
+        return lax.rem(z + ahead, Z) * per_z + lax.rem(k + y, per_z)
+
     col_id = iota((128, R), 1).astype(F32)
     for k in range(half):
-        column = as_column(cidx[pl.ds(half * c + k, 1), :])
+        column = as_column(cidx[pl.ds(back_row(k), 1), :])
         sel[k * 128:(k + 1) * 128, :] = onehot(column == col_id)
 
     @pl.when(jnp.logical_not(handler))
@@ -273,7 +297,7 @@
         drain(xall.at[0, lower], xr.at[0])
 
     for d in range(1, Y):
-        send(xall.at[y, lower], xall.at[y, lower], xs.at[2], xr.at[2], (seq_of(z, lax.rem(y + d, Y), c), x))
+        send(xall.at[unit, lower], xall.at[unit, lower], xs.at[2], xr.at[2], (seq_of(z, lax.rem(y + d, Y), c), x))
 
     @pl.when(jnp.logical_not(handler))
     def _():
@@ -289,10 +313,15 @@
             u = i * X + x
             send(xall.at[u, upper], xall.at[u, upper], xs.at[3], xr.at[3], (s, lax.rem(x + d, X)))
 
-    if X > 1:
-        send(tok, tall.at[x], tks.at[0], tkr.at[0], (s, right))
-    if X > 2:
-        send(tok, tall.at[x], tks.at[1], tkr.at[1], (s, left))
+    if X > 2:
+        drain(tall.at[0, front], tkr.at[0])
+        send(tall.at[left, front], tall.at[left, front], tks.at[2], tkr.at[2], (s, right))
+        drain(tall.at[0, back], tkr.at[1])
+        send(tall.at[right, back], tall.at[right, back], tks.at[3], tkr.at[3], (s, left))
+        send(tok.at[back], tall.at[x, back], tks.at[4], tkr.at[4], (s, right))
+        send(tok.at[front], tall.at[x, front], tks.at[5], tkr.at[5], (s, left))
+    elif X > 1:
+        drain(tall.at[0], tkr.at[0])
 
     @pl.when(c == 0)
     def _():
@@ -316,24 +345,19 @@
 
     projected(0)
 
+    @pl.when(c == 0)
+    def _():
+        for d in others:
+            zt = lax.rem(z + d, Z)
+            send(part.at[zt, pl.ds(0, 1)], rsum.at[z, pl.ds(0, 1)], rs, rr, (seq_of(zt, y, c), x))
+
     @pl.when(c == 1)
     def _():
         projected(1)
-
-    def sum_out(i, _):
-        zt = lax.rem(z + 1 + i, Z)
-
-        @pl.when(c == 0)
-        def _():
-            send(part.at[zt, pl.ds(0, 1)], rsum.at[z, pl.ds(0, 1)], rs, rr, (seq_of(zt, y, c), x))
-
-        @pl.when(c == 1)
-        def _():
+        for d in others:
+            zt = lax.rem(z + d, Z)
             send(part.at[zt], rsum.at[z], rs, rr, (seq_of(zt, y, c), x))
 
-        return 0
-
-    lax.fori_loop(0, Z - 1, sum_out, 0)
     rsum[pl.ds(z, 1), 0:1] = part[pl.ds(z, 1), 0:1]
 
     @pl.when(c == 1)
@@ -355,15 +379,6 @@
 
     project_light(tok, x, True)
 
-    th = T // 2
-    front, back = pl.ds(0, th), pl.ds(th, th)
-    if X > 1:
-        drain(tall.at[0], tkr.at[0])
-    if X > 2:
-        send(tall.at[left, front], tall.at[left, front], tks.at[2], tkr.at[2], (s, right))
-        drain(tall.at[0], tkr.at[1])
-        send(tall.at[right, back], tall.at[right, back], tks.at[3], tkr.at[3], (s, left))
-
     @pl.when(c == 0)
     def _():
         drain(rsum.at[pl.ds(0, Z - 1), pl.ds(0, 1)], rr)
@@ -380,25 +395,21 @@
             for g in range(2):
                 kv[g, i, pl.ds(z, 1)] = rows[:, g * HD:(g + 1) * HD].reshape(1, rz, HD)
 
-        def kv_zero(i, _):
-            zt = lax.rem(z + i, Z)
+        for d in [*others, 0]:
+            zt = lax.rem(z + d, Z)
             send(kv.at[0, :, z], kv.at[1, :, z], kvs, kvr, (seq_of(zt, y, 0), x))
-            return 0
-
-        def kv_one(i, _):
-            zt = lax.rem(z + 1 + i, Z)
-            send(kv.at[1, :, z], kv.at[1, :, z], kvs, kvr, (seq_of(zt, y, 1), x))
-            return 0
-
-        lax.fori_loop(0, Z, kv_zero, 0)
-        lax.fori_loop(0, Z - 1, kv_one, 0)
-
+            if d:
+                send(kv.at[1, :, z], kv.at[1, :, z], kvs, kvr, (seq_of(zt, y, 1), x))
+
+    if X > 2:
+        drain(tall.at[0, front], tkr.at[2])
+        drain(tall.at[0, back], tkr.at[3])
+        drain(tall.at[0, back], tkr.at[4])
+        drain(tall.at[0, front], tkr.at[5])
     if X > 1:
         project_light(tall.at[left], left, False)
     if X > 2:
         project_light(tall.at[right], right, False)
-        drain(tall.at[0, front], tkr.at[2])
-        drain(tall.at[0, back], tkr.at[3])
         project_light(tall.at[far], far, False)
 
     for g in range(2):
@@ -438,14 +449,16 @@
     heads = softmax_value(qbuf[0], kv[1, 0].reshape(R, HD), kv[1, 1].reshape(R, HD))
     oz[pl.ds(z, 1)] = heads.reshape(1, rz, HD)
 
-    def heads_out(i, _):
-        zt = lax.rem(z + 1 + i, Z)
+    for d in others:
+        zt = lax.rem(z + d, Z)
         send(oz.at[z], oz.at[z], ozs, ozr, (seq_of(zt, y, c), x))
-        return 0
-
-    lax.fori_loop(0, Z - 1, heads_out, 0)
+
     lacc[...] = light_out(x)
 
+    drain(oz.at[pl.ds(0, Z - 1)], ozr)
+    for d in range(1, Y):
+        send(oz, oy.at[y], oys, oyr, (seq_of(z, lax.rem(y + d, Y), c), x))
+    oy[pl.ds(y, 1)] = oz[...].reshape(1, Z, rz, HD)
     if X > 2:
         drain(lfar.at[0], lfr.at[0])
         lsend[0, :th] = (lsend[0, :th].astype(F32) + lfar[0].astype(F32)).astype(BF)
@@ -454,10 +467,6 @@
         lsend[1, th:] = (lsend[1, th:].astype(F32) + lfar[1].astype(F32)).astype(BF)
         send(lsend.at[1, back], lrecv.at[1, back], lrs, lrr, (s, left))
 
-    drain(oz.at[pl.ds(0, Z - 1)], ozr)
-    for d in range(1, Y):
-        send(oz, oy.at[y], oys, oyr, (seq_of(z, lax.rem(y + d, Y), c), x))
-    oy[pl.ds(y, 1)] = oz[...].reshape(1, Z, rz, HD)
     drain(wcat.at[pl.ds(0, FB // 2)], wor)
     if Y > 1:
         drain(oy.at[pl.ds(0, Y - 1)], oyr)
@@ -468,29 +477,34 @@
     rmine[...] = total.astype(BF)
     send(rmine, rother, cs, cr, twin)
     drain(rother, cr)
+    drain(rmine, cs)
     both = (total + rother[...].astype(F32)).astype(BF)
-    rsel[...] = dot(sel[...], both).astype(BF).reshape(S // 2, slots, FB)
+    rmine[...] = both
 
     block = pl.ds(pl.multiple_of(((z % 2) * Y + y) * FB, FB), FB)
     xq = z // 2
 
-    def give(i, _):
-        n = lax.rem(i + s + x * Y, S // 2)
-        st = (S // 2) * c + n
-        here = jnp.logical_and(st == s, xq == x)
-
-        @pl.when(jnp.logical_not(here))
-        def _():
-            send(rsel.at[n], ret.at[x, :, block], rts, rtr, (st, xq))
+    step = S // 2 // half
+
+    def choose(k, _):
+        chosen = dot(sel[pl.ds(pl.multiple_of(k * 128, 128), 128), :], rmine[...]).astype(BF)
+        rsel[pl.ds(k * step, step)] = chosen.reshape(step, slots, FB)
+        for i in range(step):
+            st = back_row(k) * step + i
+            here = jnp.logical_and(st == s, xq == x)
+
+            @pl.when(jnp.logical_not(here))
+            def _():
+                send(rsel.at[k * step + i], ret.at[x, :, block], rts, rtr, (st, xq))
+
+            @pl.when(here)
+            def _():
+                ret[pl.ds(x, 1), :, block] = rsel[pl.ds(k * step + i, 1)]
 
         return 0
 
-    lax.fori_loop(0, S // 2, give, 0)
-    keeps = jnp.logical_and(xq == x, s // (S // 2) == c)
-
-    @pl.when(keeps)
-    def _():
-        ret[pl.ds(x, 1), :, block] = rsel[pl.ds(lax.rem(s, S // 2), 1)]
+    lax.fori_loop(0, half, choose, 0)
+    keeps = jnp.logical_and(xq == x, c == 0)
 
     if X > 2:
         drain(lrecv, lrr)
@@ -517,7 +531,7 @@
     if X > 1:
         drain(planes.at[:, pl.ds(0, X - 1)], s0s)
         drain(xall.at[pl.ds(0, NY * (X - 1)), upper], xs.at[3])
-        drain(tall.at[0], tks.at[0])
+        drain(tall.at[0, front] if X > 2 else tall.at[0], tks.at[0])
 
     @pl.when(handler)
     def _():
@@ -545,7 +559,9 @@
 
     drain(wcat.at[pl.ds(0, FB // 2)], wos)
     if X > 2:
-        drain(tall.at[0], tks.at[1])
+        drain(tall.at[0, back], tks.at[1])
+        drain(tall.at[0, back], tks.at[4])
+        drain(tall.at[0, front], tks.at[5])
         drain(tall.at[0, front], tks.at[2])
         drain(tall.at[0, back], tks.at[3])
         drain(lsend, lrs)
@@ -567,7 +583,6 @@
         drain(kv.at[0, :, pl.ds(0, Z - 1)], kvs)
 
     drain(oz.at[pl.ds(0, Z - 1)], ozs)
-    drain(rmine, cs)
 
     @pl.when(keeps)
     def _():
@@ -626,7 +641,7 @@
         pltpu.VMEM((T, FX), F32),
         pltpu.VMEM((S * slots // 128, 128), F32),
         *[dma(()) for _ in range(26)],
-        dma((4,)), dma((4,)), dma((4,)), dma((4,)), dma((2,)), dma((6,)),
+        dma((6,)), dma((6,)), dma((4,)), dma((4,)), dma((2,)), dma((6,)),
     ]
     return pl.pallas_call(
         functools.partial(kernel, dims),
@@ -634,10 +649,13 @@
         in_specs=[hbm] * 8,
         out_specs=pl.BlockSpec(memory_space=pltpu.VMEM),
         scratch_shapes=scratch,
-        compiler_params=pltpu.CompilerParams(collective_id=0, has_side_effects=True, vmem_limit_bytes=56 << 20),
-    )(
-        tokens, light_input, light_output, heavy_input, heavy_output.T, query_tokens.T, context_tokens.T, query_gate
-    )
+        compiler_params=pltpu.CompilerParams(collective_id=0, has_side_effects=True, vmem_limit_bytes=48 << 20),
+    )(*(
+        pltpu.with_memory_space_constraint(a, pltpu.HBM)
+        for a in (
+            tokens, light_input, light_output, heavy_input, heavy_output.T, query_tokens.T, context_tokens.T, query_gate
+        )
+    ))
 
 
 def solution(mesh):

time: 84.6 us -> 78 us (0.922)
  the two profiles are of different devices: /device:TPU:37 before, /device:TPU:1 now
where the time goes in v3:
time: 78 us; the launch traced here: 77.8 us
  Pallas kernels  77 us (99%)
  local copies, waits for them, and re-layouts  0.8 us (1%)
    pallas_call x1, Pallas kernels, body(): pl.pallas_call(functools.partial(kernel, dims), out_shape=jax.ShapeDtypeS...  77 us

profile of v3, /device:TPU:1, one launch (start us, length us, event | category | flops | bytes accessed | tf_op | source)
XLA Modules:
  0.0 77.8 jit_solution(10095868208449516416)
XLA Ops:
  0.0 77.0 %shard_map.82 = bf16[256,1024]{1,0:T(8,128)(2,1)S(1)} custom-call(bf16[256,1024]{1,0:T(8,128)(2,1)} %tok_any.1, bf16[3,4096,256]{2,1,0:T(8,128)(2,1)} %lin.1, bf16[256,4096]{1,0:T(8,128)(2,1)} %lout.1, bf16[3,64,1024]{2,1,0:T(8,128)(2,1)} %hin_any.1, bf16[64,1024]{1,0:T(8,128)(2,1)} %bitcast.3, s32[32,64]{1,0:T(8,128)} %bitcast.4, s32[32,64]{1,0:T(8,128)} %bitcast.5, ...), custom_call_target="tpu_custom_call" | custom-call | tf_op jit(solution)/shard_map/pallas_call | solution.py:646
  77.0 0.8 %copy.10 = bf16[256,1024]{1,0:T(8,128)(2,1)} copy(bf16[256,1024]{1,0:T(8,128)(2,1)S(1)} %shard_map.82) | data formatting | bytes 1048576

commit v4 on v3

--- a/solution.py
+++ b/solution.py
@@ -72,12 +72,12 @@
     tok_any, lin, lout, hin_any, hout_any, qtab_any, ctab_any, gate_any,
     out,
     tok, hin, hout, qtab, ctab, gate,
-    picks, planes, landed, comp, sel, xall, wbuf, part, rsum, kv, qbuf, oz, oy,
+    picks, planes, landed, comp, sel, xall, wbuf, part, rsum, kv, qbuf, oy,
     wcat, rmine, rother, rsel, ret,
     tall, lw, lo, lmap, lheads, lsend, lfar, lrecv, lacc, cidx,
-    s0s, s0r, s1s, s1r, wss, wsr, wos, wor, rs, rr, kvs, kvr, qs, qr,
-    ozs, ozr, oys, oyr, cs, cr, rts, rtr, lrs, lrr, lis, los,
-    tks, tkr, xs, xr, lfr, ins,
+    s0s, s0r, s1s, s1r, wss, wsr, wos, wor, qs, qr,
+    ozs, oys, oyr, cs, cr, rts, rtr, lrs, lrr, lis, los,
+    tks, tkr, xs, xr, lfr, ins, rs, rr, kvs, kvr, ozr,
 ):
     Z, Y, X = dims
     NY = Y // X
@@ -259,25 +259,34 @@
         for k in range(krows):
             comp[:, k * 128:(k + 1) * 128] = onehot(row_id == mine[k:k + 1, :])
 
-    rh = R // 2
-    lower, upper = pl.ds(0, rh), pl.ds(rh, rh)
+    rq = R // 4
+    quarters = [pl.ds(i * rq, rq) for i in range(4)]
+    turns = (0, 2, 1, 3)
+    lower, upper = pl.ds(0, R // 2), pl.ds(R // 2, R // 2)
+
+    def to_row(q, u, k):
+        for d in range(1, X):
+            send(xall.at[u, quarters[q]], xall.at[u, quarters[q]], xs.at[k], xr.at[k], (s, lax.rem(x + d, X)))
+
+    def to_column(q, u, k):
+        for d in range(1, Y):
+            to = (seq_of(z, lax.rem(y + d, Y), c), x)
+            send(xall.at[u, quarters[q]], xall.at[u, quarters[q]], xs.at[k], xr.at[k], to)
 
     @pl.when(handler)
     def _():
         drain(landed.at[pl.ds(0, S - 1)], s1r)
-        for part_rows in (lower, upper):
-            xall[pl.ds(unit, 1), part_rows] = dot(
-                comp[part_rows, :], landed[...].reshape(S * slots, FB)
-            ).astype(BF).reshape(1, rh, FB)
-            if part_rows is lower:
-                for d in range(1, X):
-                    send(xall.at[unit, lower], xall.at[unit, lower], xs.at[0], xr.at[0], (s, lax.rem(x + d, X)))
+        for q in turns:
+            xall[pl.ds(unit, 1), quarters[q]] = dot(
+                comp[quarters[q], :], landed[...].reshape(S * slots, FB)
+            ).astype(BF).reshape(1, rq, FB)
+            if q < 2:
+                to_row(q, unit, q)
+                to_column(q, unit, 4)
             else:
-                for d in range(1, Y):
-                    send(
-                        xall.at[unit, upper], xall.at[unit, upper], xs.at[1], xr.at[1],
-                        (seq_of(z, lax.rem(y + d, Y), c), x),
-                    )
+                to_column(q, unit, q)
+                if NY == 1:
+                    to_row(q, unit, 5)
 
     cidx[...] = q_idx
     half = krows // 2
@@ -292,26 +301,28 @@
         column = as_column(cidx[pl.ds(back_row(k), 1), :])
         sel[k * 128:(k + 1) * 128, :] = onehot(column == col_id)
 
-    @pl.when(jnp.logical_not(handler))
-    def _():
-        drain(xall.at[0, lower], xr.at[0])
-
-    for d in range(1, Y):
-        send(xall.at[unit, lower], xall.at[unit, lower], xs.at[2], xr.at[2], (seq_of(z, lax.rem(y + d, Y), c), x))
-
-    @pl.when(jnp.logical_not(handler))
-    def _():
-        drain(xall.at[pl.ds(0, NY), lower], xr.at[1])
-
-    if NY > 1:
-        @pl.when(handler)
-        def _():
-            drain(xall.at[pl.ds(0, NY - 1), lower], xr.at[1])
-
-    for d in range(1, X):
-        for i in range(NY):
-            u = i * X + x
-            send(xall.at[u, upper], xall.at[u, upper], xs.at[3], xr.at[3], (s, lax.rem(x + d, X)))
+    for q in turns:
+        if q < 2:
+            @pl.when(jnp.logical_not(handler))
+            def _():
+                drain(xall.at[0, quarters[q]], xr.at[q])
+                to_column(q, unit, 4)
+        elif NY == 1:
+            @pl.when(jnp.logical_not(handler))
+            def _():
+                drain(xall.at[0, quarters[q]], xr.at[q])
+                to_row(q, x, 5)
+        else:
+            @pl.when(handler)
+            def _():
+                drain(xall.at[pl.ds(0, NY - 1), quarters[q]], xr.at[q])
+
+            @pl.when(jnp.logical_not(handler))
+            def _():
+                drain(xall.at[pl.ds(0, NY), quarters[q]], xr.at[q])
+
+            for i in range(NY):
+                to_row(q, i * X + x, 5)
 
     if X > 2:
         drain(tall.at[0, front], tkr.at[0])
@@ -332,9 +343,9 @@
         drain(wbuf.at[pl.ds(0, 2), pl.ds(0, nb - 1)], wsr)
 
     if Y > 1:
-        drain(xall.at[pl.ds(0, Y - 1), lower], xr.at[2])
+        drain(xall.at[pl.ds(0, Y - 1), lower], xr.at[4])
     if X > 1:
-        drain(xall.at[pl.ds(0, NY * (X - 1)), upper], xr.at[3])
+        drain(xall.at[pl.ds(0, NY * (X - 1)), upper], xr.at[5])
 
     def projected(i):
         total = None
@@ -343,26 +354,18 @@
             total = term if total is None else total + term
         part[:, i] = total.astype(BF).reshape(Z, rz, 2 * HD)
 
-    projected(0)
-
-    @pl.when(c == 0)
-    def _():
+    def sum_out(i):
+        projected(i)
         for d in others:
             zt = lax.rem(z + d, Z)
-            send(part.at[zt, pl.ds(0, 1)], rsum.at[z, pl.ds(0, 1)], rs, rr, (seq_of(zt, y, c), x))
+            send(part.at[zt, i], rsum.at[z, i], rs.at[i], rr.at[i], (seq_of(zt, y, c), x))
+        rsum[pl.ds(z, 1), i:i + 1] = part[pl.ds(z, 1), i:i + 1]
+
+    sum_out(0)
 
     @pl.when(c == 1)
     def _():
-        projected(1)
-        for d in others:
-            zt = lax.rem(z + d, Z)
-            send(part.at[zt], rsum.at[z], rs, rr, (seq_of(zt, y, c), x))
-
-    rsum[pl.ds(z, 1), 0:1] = part[pl.ds(z, 1), 0:1]
-
-    @pl.when(c == 1)
-    def _():
-        rsum[pl.ds(z, 1), 1:2] = part[pl.ds(z, 1), 1:2]
+        sum_out(1)
 
     load_in.wait()
 
@@ -379,27 +382,31 @@
 
     project_light(tok, x, True)
 
-    @pl.when(c == 0)
-    def _():
-        drain(rsum.at[pl.ds(0, Z - 1), pl.ds(0, 1)], rr)
-        rows = jnp.sum(rsum[:, 0].astype(F32), axis=0).astype(BF)
-        qbuf[0] = rows[:, :HD]
-        qbuf[1] = rows[:, HD:]
-        send(qbuf.at[1], qbuf.at[0], qs, qr, twin)
-
-    @pl.when(c == 1)
-    def _():
-        drain(rsum.at[pl.ds(0, Z - 1)], rr)
-        for i in range(2):
-            rows = jnp.sum(rsum[:, i].astype(F32), axis=0).astype(BF)
-            for g in range(2):
-                kv[g, i, pl.ds(z, 1)] = rows[:, g * HD:(g + 1) * HD].reshape(1, rz, HD)
-
+    def summed(i):
+        drain(rsum.at[pl.ds(0, Z - 1), 0], rr.at[i])
+        return jnp.sum(rsum[:, i].astype(F32), axis=0).astype(BF)
+
+    def kv_out(i):
+        total = summed(i)
+        for g in range(2):
+            kv[g, i, pl.ds(z, 1)] = total[:, g * HD:(g + 1) * HD].reshape(1, rz, HD)
         for d in [*others, 0]:
             zt = lax.rem(z + d, Z)
-            send(kv.at[0, :, z], kv.at[1, :, z], kvs, kvr, (seq_of(zt, y, 0), x))
+            send(kv.at[0, i, z], kv.at[1, i, z], kvs.at[i], kvr.at[i], (seq_of(zt, y, 0), x))
             if d:
-                send(kv.at[1, :, z], kv.at[1, :, z], kvs, kvr, (seq_of(zt, y, 1), x))
+                send(kv.at[1, i, z], kv.at[1, i, z], kvs.at[i], kvr.at[i], (seq_of(zt, y, 1), x))
+
+    @pl.when(c == 0)
+    def _():
+        total = summed(0)
+        qbuf[0] = total[:, :HD]
+        qbuf[1] = total[:, HD:]
+        send(qbuf.at[1], qbuf.at[0], qs, qr, twin)
+
+    @pl.when(c == 1)
+    def _():
+        kv_out(0)
+        kv_out(1)
 
     if X > 2:
         drain(tall.at[0, front], tkr.at[2])
@@ -437,28 +444,40 @@
     elif X > 1:
         send(lsend.at[0], lrecv.at[0], lrs, lrr, (s, right))
 
-    @pl.when(c == 0)
-    def _():
-        drain(kv.at[1], kvr)
+    def arrived(i):
+        @pl.when(c == 0)
+        def _():
+            drain(kv.at[1, 0], kvr.at[i])
+
+        @pl.when(c == 1)
+        def _():
+            drain(kv.at[1, 0, pl.ds(0, Z - 1)], kvr.at[i])
 
     @pl.when(c == 1)
     def _():
         drain(qbuf.at[0], qr)
-        drain(kv.at[1, :, pl.ds(0, Z - 1)], kvr)
-
-    heads = softmax_value(qbuf[0], kv[1, 0].reshape(R, HD), kv[1, 1].reshape(R, HD))
-    oz[pl.ds(z, 1)] = heads.reshape(1, rz, HD)
-
+
+    arrived(0)
+    scores = dot_nt(qbuf[0], kv[1, 0].reshape(R, HD)) * (1.0 / math.sqrt(HD))
+    expanded = jnp.exp(scores - jnp.max(scores, axis=-1, keepdims=True))
+    totals = jnp.sum(expanded, axis=-1, keepdims=True)
+    arrived(1)
+    heads = (dot(expanded.astype(BF), kv[1, 1].reshape(R, HD)) / totals).astype(BF)
+    oy[pl.ds(y, 1), pl.ds(z, 1)] = heads.reshape(1, 1, rz, HD)
     for d in others:
         zt = lax.rem(z + d, Z)
-        send(oz.at[z], oz.at[z], ozs, ozr, (seq_of(zt, y, c), x))
-
+        send(oy.at[y, z], oy.at[y, z], ozs, ozr.at[d], (seq_of(zt, y, c), x))
+
+    def heads_over_y(zz):
+        for d in range(1, Y):
+            send(oy.at[y, zz], oy.at[y, zz], oys, oyr, (seq_of(z, lax.rem(y + d, Y), c), x))
+
+    heads_over_y(z)
     lacc[...] = light_out(x)
-
-    drain(oz.at[pl.ds(0, Z - 1)], ozr)
-    for d in range(1, Y):
-        send(oz, oy.at[y], oys, oyr, (seq_of(z, lax.rem(y + d, Y), c), x))
-    oy[pl.ds(y, 1)] = oz[...].reshape(1, Z, rz, HD)
+    for d in reversed(others):
+        drain(oy.at[0, 0], ozr.at[d])
+        heads_over_y(lax.rem(z + Z - d, Z))
+
     if X > 2:
         drain(lfar.at[0], lfr.at[0])
         lsend[0, :th] = (lsend[0, :th].astype(F32) + lfar[0].astype(F32)).astype(BF)
@@ -530,16 +549,18 @@
 
     if X > 1:
         drain(planes.at[:, pl.ds(0, X - 1)], s0s)
-        drain(xall.at[pl.ds(0, NY * (X - 1)), upper], xs.at[3])
+        drain(xall.at[pl.ds(0, NY * (X - 1)), upper], xs.at[5])
         drain(tall.at[0, front] if X > 2 else tall.at[0], tks.at[0])
 
     @pl.when(handler)
     def _():
         drain(landed.at[pl.ds(0, fan - 1)], s1s)
         if X > 1:
-            drain(xall.at[pl.ds(0, X - 1), lower], xs.at[0])
+            for q in range(2):
+                drain(xall.at[pl.ds(0, X - 1), quarters[q]], xs.at[q])
         if Y > 1:
-            drain(xall.at[pl.ds(0, Y - 1), upper], xs.at[1])
+            for q in range(2, 4):
+                drain(xall.at[pl.ds(0, Y - 1), quarters[q]], xs.at[q])
 
     @pl.when(jnp.logical_not(handler))
     def _():
@@ -568,21 +589,23 @@
     elif X > 1:
         drain(lsend.at[0], lrs)
     if Y > 1:
-        drain(xall.at[pl.ds(0, Y - 1), lower], xs.at[2])
+        drain(xall.at[pl.ds(0, Y - 1), lower], xs.at[4])
         drain(oy.at[pl.ds(0, Y - 1)], oys)
 
+    drain(rsum.at[pl.ds(0, Z - 1), 0], rs.at[0])
+
     @pl.when(c == 0)
     def _():
-        drain(rsum.at[pl.ds(0, Z - 1), pl.ds(0, 1)], rs)
         drain(qbuf.at[0], qs)
 
     @pl.when(c == 1)
     def _():
-        drain(rsum.at[pl.ds(0, Z - 1)], rs)
-        drain(kv.at[0], kvs)
-        drain(kv.at[0, :, pl.ds(0, Z - 1)], kvs)
-
-    drain(oz.at[pl.ds(0, Z - 1)], ozs)
+        drain(rsum.at[pl.ds(0, Z - 1), 0], rs.at[1])
+        for i in range(2):
+            drain(kv.at[0, 0], kvs.at[i])
+            drain(kv.at[0, 0, pl.ds(0, Z - 1)], kvs.at[i])
+
+    drain(oy.at[0, pl.ds(0, Z - 1)], ozs)
 
     @pl.when(keeps)
     def _():
@@ -623,7 +646,6 @@
         pltpu.VMEM((Z, 2, rz, 2 * HD), BF),
         pltpu.VMEM((2, 2, Z, rz, HD), BF),
         pltpu.VMEM((2, rz, HD), BF),
-        pltpu.VMEM((Z, rz, HD), BF),
         pltpu.VMEM((Y, Z, rz, HD), BF),
         pltpu.VMEM((FB, Y * HD), BF),
         pltpu.VMEM((R, FB), BF),
@@ -640,8 +662,9 @@
         pltpu.VMEM((2, T, FX), BF),
         pltpu.VMEM((T, FX), F32),
         pltpu.VMEM((S * slots // 128, 128), F32),
-        *[dma(()) for _ in range(26)],
-        dma((6,)), dma((6,)), dma((4,)), dma((4,)), dma((2,)), dma((6,)),
+        *[dma(()) for _ in range(21)],
+        dma((6,)), dma((6,)), dma((6,)), dma((6,)), dma((2,)), dma((6,)),
+        dma((2,)), dma((2,)), dma((2,)), dma((2,)), dma((Z,)),
     ]
     return pl.pallas_call(
         functools.partial(kernel, dims),

time: 78 us -> 74.9 us (0.960)
  Pallas kernels: 77 us -> 73.9 us
    pallas_call x1, Pallas kernels: 77 us -> 73.9 us  [body(): pl.pallas_call(functools.partial(kernel, dims), out_shape=jax.ShapeDtypeS...]
where the time goes in v4:
time: 74.9 us; the launch traced here: 74.7 us
  Pallas kernels  73.9 us (99%)
  local copies, waits for them, and re-layouts  0.8 us (1%)
    pallas_call x1, Pallas kernels, body(): pl.pallas_call(functools.partial(kernel, dims), out_shape=jax.ShapeDtypeS...  73.9 us

profile of v4, /device:TPU:1, one launch (start us, length us, event | category | flops | bytes accessed | tf_op | source)
XLA Modules:
  0.0 74.7 jit_solution(14119344933288239373)
XLA Ops:
  0.0 73.9 %shard_map.82 = bf16[256,1024]{1,0:T(8,128)(2,1)S(1)} custom-call(bf16[256,1024]{1,0:T(8,128)(2,1)} %tok_any.1, bf16[3,4096,256]{2,1,0:T(8,128)(2,1)} %lin.1, bf16[256,4096]{1,0:T(8,128)(2,1)} %lout.1, bf16[3,64,1024]{2,1,0:T(8,128)(2,1)} %hin_any.1, bf16[64,1024]{1,0:T(8,128)(2,1)} %bitcast.3, s32[32,64]{1,0:T(8,128)} %bitcast.4, s32[32,64]{1,0:T(8,128)} %bitcast.5, ...), custom_call_target="tpu_custom_call" | custom-call | tf_op jit(solution)/shard_map/pallas_call | solution.py:669
  73.9 0.8 %copy.10 = bf16[256,1024]{1,0:T(8,128)(2,1)} copy(bf16[256,1024]{1,0:T(8,128)(2,1)S(1)} %shard_map.82) | data formatting | bytes 1048576

commit v5 on v4

--- a/solution.py
+++ b/solution.py
@@ -72,8 +72,8 @@
     tok_any, lin, lout, hin_any, hout_any, qtab_any, ctab_any, gate_any,
     out,
     tok, hin, hout, qtab, ctab, gate,
-    picks, planes, landed, comp, sel, xall, wbuf, part, rsum, kv, qbuf, oy,
-    wcat, rmine, rother, rsel, ret,
+    picks, planes, landed, comp, sel, xall, wbuf, part, rsum, kv, qbuf, hmine, oh,
+    wy, psend, precv, rfull, rsel, ret,
     tall, lw, lo, lmap, lheads, lsend, lfar, lrecv, lacc, cidx,
     s0s, s0r, s1s, s1r, wss, wsr, wos, wor, qs, qr,
     ozs, oys, oyr, cs, cr, rts, rtr, lrs, lrr, lis, los,
@@ -111,28 +111,6 @@
     def drain(ref, sem):
         pltpu.make_async_copy(ref, ref, sem).wait()
 
-    barrier = pltpu.get_barrier_semaphore()
-
-    def greet(to):
-        pl.semaphore_signal(barrier, inc=1, device_id=to, device_id_type=pl.DeviceIdType.MESH)
-
-    unit = (y + c * (Y // 2)) % Y
-    handler = unit % X == x
-
-    for d in range(1, nb):
-        jt = lax.rem(2 * y + c + d, nb)
-        greet((seq_of(z, jt // 2, jt % 2), x))
-    for d in range(1, X):
-        greet((s, lax.rem(x + d, X)))
-
-    @pl.when(handler)
-    def _():
-        def greet_plane(i, _):
-            greet((lax.rem(s + 1 + i, S), x))
-            return 0
-
-        lax.fori_loop(0, S - 1, greet_plane, 0)
-
     fetches = [
         pltpu.make_async_copy(src, dst, ins.at[i])
         for i, (src, dst) in enumerate((
@@ -143,8 +121,31 @@
         fetch.start()
     load_in = pltpu.make_async_copy(lin, lw, lis)
     load_out = pltpu.make_async_copy(lout, lo, los)
-    load_in.start()
-    load_out.start()
+    barrier = pltpu.get_barrier_semaphore()
+
+    def greet(to):
+        pl.semaphore_signal(barrier, inc=1, device_id=to, device_id_type=pl.DeviceIdType.MESH)
+
+    unit = (y + c * (Y // 2)) % Y
+    handler = unit % X == x
+    zh = Z // 2
+    zi = z % zh
+    keeper = z // zh
+    owns = keeper == c
+
+    for d in range(1, nb):
+        jt = lax.rem(2 * y + c + d, nb)
+        greet((seq_of(z, jt // 2, jt % 2), x))
+    for d in range(1, X):
+        greet((s, lax.rem(x + d, X)))
+
+    @pl.when(handler)
+    def _():
+        def greet_plane(i, _):
+            greet((lax.rem(s + 1 + i, S), x))
+            return 0
+
+        lax.fori_loop(0, S - 1, greet_plane, 0)
 
     fetches[0].wait()
     fetches[1].wait()
@@ -175,12 +176,9 @@
     for i in range(NY):
         planes[i, pl.ds(x, 1)] = picks[pl.ds(i * X + x, 1)]
 
-    mine_rows = pl.ds(pl.multiple_of(c * (FB // 2), FB // 2), FB // 2)
     fetches[3].wait()
     fetches[4].wait()
     fetches[5].wait()
-    for yy in range(Y):
-        wcat[mine_rows, yy * HD:(yy + 1) * HD] = hout[:, pl.ds(pl.multiple_of((2 * yy + c) * HD, HD), HD)]
     if X > 1:
         drain(planes.at[:, pl.ds(0, X - 1)], s0r)
 
@@ -207,6 +205,9 @@
             pl.ds(unit // X, 1), pl.ds(z // 2, 1), pl.ds(z % 2, 1), pl.ds(c, 1)
         ].reshape(1, slots, FB)
 
+    load_in.start()
+    load_out.start()
+
     th = T // 2
     front, back = pl.ds(0, th), pl.ds(th, th)
     if X > 2:
@@ -244,9 +245,12 @@
     def _():
         wbuf[pl.ds(0, 2), pl.ds(j, 1)] = hin[pl.ds(1, 2), :, own_cols].reshape(2, 1, hin.shape[1], 2 * HD)
 
-    for yy in range(Y):
-        theirs = pl.ds(pl.multiple_of((2 * yy + 1 - c) * HD, HD), HD)
-        send(hout.at[:, theirs], wcat.at[mine_rows, pl.ds(yy * HD, HD)], wos, wor, twin)
+    wrows = pl.ds(pl.multiple_of(j * (FB // 2), FB // 2), FB // 2)
+    for d in range(1, nb):
+        jt = lax.rem(j + d, nb)
+        cols = pl.ds(pl.multiple_of(jt // 2 * 2 * HD, 2 * HD), 2 * HD)
+        send(hout.at[:, cols], wy.at[wrows, :], wos, wor, (seq_of(z, jt // 2, jt % 2), x))
+    wy[wrows, :] = hout[:, own_cols]
 
     q_idx = compact_index(qtab[...])
     c_idx = compact_index(ctab[...])
@@ -260,9 +264,9 @@
             comp[:, k * 128:(k + 1) * 128] = onehot(row_id == mine[k:k + 1, :])
 
     rq = R // 4
+    rt = rq // Z
     quarters = [pl.ds(i * rq, rq) for i in range(4)]
     turns = (0, 2, 1, 3)
-    lower, upper = pl.ds(0, R // 2), pl.ds(R // 2, R // 2)
 
     def to_row(q, u, k):
         for d in range(1, X):
@@ -282,11 +286,11 @@
             ).astype(BF).reshape(1, rq, FB)
             if q < 2:
                 to_row(q, unit, q)
-                to_column(q, unit, 4)
+                to_column(q, unit, 4 + q)
             else:
                 to_column(q, unit, q)
                 if NY == 1:
-                    to_row(q, unit, 5)
+                    to_row(q, unit, 4 + q)
 
     cidx[...] = q_idx
     half = krows // 2
@@ -296,7 +300,10 @@
         ahead = jnp.where(c == 0, Z // 2 - 1 - k // per_z, Z // 2 + k // per_z)
         return lax.rem(z + ahead, Z) * per_z + lax.rem(k + y, per_z)
 
-    col_id = iota((128, R), 1).astype(F32)
+    held = iota((128, R), 1)
+    place = held % rz // rt
+    quarter = jnp.where(place == 1, 2, jnp.where(place == 2, 1, place))
+    col_id = (quarter * rq + held // rz * rt + held % rt).astype(F32)
     for k in range(half):
         column = as_column(cidx[pl.ds(back_row(k), 1), :])
         sel[k * 128:(k + 1) * 128, :] = onehot(column == col_id)
@@ -306,12 +313,12 @@
             @pl.when(jnp.logical_not(handler))
             def _():
                 drain(xall.at[0, quarters[q]], xr.at[q])
-                to_column(q, unit, 4)
+                to_column(q, unit, 4 + q)
         elif NY == 1:
             @pl.when(jnp.logical_not(handler))
             def _():
                 drain(xall.at[0, quarters[q]], xr.at[q])
-                to_row(q, x, 5)
+                to_row(q, x, 4 + q)
         else:
             @pl.when(handler)
             def _():
@@ -322,7 +329,7 @@
                 drain(xall.at[pl.ds(0, NY), quarters[q]], xr.at[q])
 
             for i in range(NY):
-                to_row(q, i * X + x, 5)
+                to_row(q, i * X + x, 4 + q)
 
     if X > 2:
         drain(tall.at[0, front], tkr.at[0])
@@ -342,30 +349,41 @@
     def _():
         drain(wbuf.at[pl.ds(0, 2), pl.ds(0, nb - 1)], wsr)
 
-    if Y > 1:
-        drain(xall.at[pl.ds(0, Y - 1), lower], xr.at[4])
-    if X > 1:
-        drain(xall.at[pl.ds(0, NY * (X - 1)), upper], xr.at[5])
-
-    def projected(i):
+    def there(q):
+        if q < 2 and Y > 1:
+            drain(xall.at[pl.ds(0, Y - 1), quarters[q]], xr.at[4 + q])
+        if q >= 2 and X > 1:
+            drain(xall.at[pl.ds(0, NY * (X - 1)), quarters[q]], xr.at[4 + q])
+
+    def projected(i, at):
         total = None
         for yy in range(Y):
-            term = dot(xall[yy], wbuf[i, 2 * yy:2 * yy + 2].reshape(FB, 2 * HD))
+            term = dot(xall[yy, quarters[turns[at]]], wbuf[i, 2 * yy:2 * yy + 2].reshape(FB, 2 * HD))
             total = term if total is None else total + term
-        part[:, i] = total.astype(BF).reshape(Z, rz, 2 * HD)
-
-    def sum_out(i):
-        projected(i)
+        part[:, i, at * rt:(at + 1) * rt] = total.astype(BF).reshape(Z, rt, 2 * HD)
+
+    def sum_out(i, first, last):
+        rows = pl.ds(first * rt, (last - first) * rt)
+        for at in range(first, last):
+            projected(i, at)
         for d in others:
             zt = lax.rem(z + d, Z)
-            send(part.at[zt, i], rsum.at[z, i], rs.at[i], rr.at[i], (seq_of(zt, y, c), x))
-        rsum[pl.ds(z, 1), i:i + 1] = part[pl.ds(z, 1), i:i + 1]
-
-    sum_out(0)
+            send(part.at[zt, i, rows], rsum.at[z, i, rows], rs.at[i], rr.at[i], (seq_of(zt, y, c), x))
+
+    for h in range(2):
+        there(turns[2 * h])
+        there(turns[2 * h + 1])
+        sum_out(0, 2 * h, 2 * h + 2)
 
     @pl.when(c == 1)
     def _():
-        sum_out(1)
+        sum_out(1, 0, 4)
+
+    rsum[pl.ds(z, 1), 0:1] = part[pl.ds(z, 1), 0:1]
+
+    @pl.when(c == 1)
+    def _():
+        rsum[pl.ds(z, 1), 1:2] = part[pl.ds(z, 1), 1:2]
 
     load_in.wait()
 
@@ -463,20 +481,41 @@
     totals = jnp.sum(expanded, axis=-1, keepdims=True)
     arrived(1)
     heads = (dot(expanded.astype(BF), kv[1, 1].reshape(R, HD)) / totals).astype(BF)
-    oy[pl.ds(y, 1), pl.ds(z, 1)] = heads.reshape(1, 1, rz, HD)
+    heads_at = (pl.ds(pl.multiple_of(zi * rz, rz), rz), pl.ds(pl.multiple_of(c * HD, HD), HD))
+    hmine[...] = heads
+
+    @pl.when(owns)
+    def _():
+        oh[heads_at] = heads
+
     for d in others:
-        zt = lax.rem(z + d, Z)
-        send(oy.at[y, z], oy.at[y, z], ozs, ozr.at[d], (seq_of(zt, y, c), x))
-
-    def heads_over_y(zz):
+        send(hmine, oh.at[heads_at], ozs, ozr, (seq_of(lax.rem(z + d, Z), y, keeper), x))
+
+    @pl.when(jnp.logical_not(owns))
+    def _():
+        send(hmine, oh.at[heads_at], ozs, ozr, twin)
+
+    lacc[...] = light_out(x)
+    drain(wy.at[pl.ds(0, (nb - 1) * (FB // 2))], wor)
+
+    @pl.when(owns)
+    def _():
+        drain(rsel.at[pl.ds(0, (Z - 1) * rz // slots)], ozr)
+
+    @pl.when(jnp.logical_not(owns))
+    def _():
+        drain(oh, ozr)
+
+    ph = zh * rz // 2
+    for h in range(2):
+        rows = pl.ds(h * ph, ph)
+        product = dot_nt(oh[rows, :], wy[...]).astype(BF)
+        for yy in range(Y):
+            psend[yy, rows] = product[:, yy * FB:(yy + 1) * FB]
         for d in range(1, Y):
-            send(oy.at[y, zz], oy.at[y, zz], oys, oyr, (seq_of(z, lax.rem(y + d, Y), c), x))
-
-    heads_over_y(z)
-    lacc[...] = light_out(x)
-    for d in reversed(others):
-        drain(oy.at[0, 0], ozr.at[d])
-        heads_over_y(lax.rem(z + Z - d, Z))
+            yt = lax.rem(y + d, Y)
+            send(psend.at[yt, rows], precv.at[y, rows], oys, oyr, (seq_of(z, yt, c), x))
+        precv[pl.ds(y, 1), rows] = psend[pl.ds(y, 1), rows]
 
     if X > 2:
         drain(lfar.at[0], lfr.at[0])
@@ -486,19 +525,11 @@
         lsend[1, th:] = (lsend[1, th:].astype(F32) + lfar[1].astype(F32)).astype(BF)
         send(lsend.at[1, back], lrecv.at[1, back], lrs, lrr, (s, left))
 
-    drain(wcat.at[pl.ds(0, FB // 2)], wor)
     if Y > 1:
-        drain(oy.at[pl.ds(0, Y - 1)], oyr)
-    total = None
-    for yy in range(Y):
-        term = dot_nt(oy[yy].reshape(R, HD), wcat[:, yy * HD:(yy + 1) * HD])
-        total = term if total is None else total + term
-    rmine[...] = total.astype(BF)
-    send(rmine, rother, cs, cr, twin)
-    drain(rother, cr)
-    drain(rmine, cs)
-    both = (total + rother[...].astype(F32)).astype(BF)
-    rmine[...] = both
+        drain(precv.at[pl.ds(0, Y - 1)], oyr)
+    rfull[pl.ds(c, 1)] = jnp.sum(precv[...].astype(F32), axis=0).astype(BF).reshape(1, zh * rz, FB)
+    send(rfull.at[c], rfull.at[c], cs, cr, twin)
+    drain(rfull.at[0], cr)
 
     block = pl.ds(pl.multiple_of(((z % 2) * Y + y) * FB, FB), FB)
     xq = z // 2
@@ -506,7 +537,7 @@
     step = S // 2 // half
 
     def choose(k, _):
-        chosen = dot(sel[pl.ds(pl.multiple_of(k * 128, 128), 128), :], rmine[...]).astype(BF)
+        chosen = dot(sel[pl.ds(pl.multiple_of(k * 128, 128), 128), :], rfull[...].reshape(R, FB)).astype(BF)
         rsel[pl.ds(k * step, step)] = chosen.reshape(step, slots, FB)
         for i in range(step):
             st = back_row(k) * step + i
@@ -549,7 +580,8 @@
 
     if X > 1:
         drain(planes.at[:, pl.ds(0, X - 1)], s0s)
-        drain(xall.at[pl.ds(0, NY * (X - 1)), upper], xs.at[5])
+        for q in (2, 3):
+            drain(xall.at[pl.ds(0, NY * (X - 1)), quarters[q]], xs.at[4 + q])
         drain(tall.at[0, front] if X > 2 else tall.at[0], tks.at[0])
 
     @pl.when(handler)
@@ -578,7 +610,8 @@
         if Y > 1:
             drain(wbuf.at[pl.ds(0, 2), pl.ds(0, Y - 1)], wss)
 
-    drain(wcat.at[pl.ds(0, FB // 2)], wos)
+    drain(wy.at[pl.ds(0, (nb - 1) * (FB // 2))], wos)
+    drain(rfull.at[0], cs)
     if X > 2:
         drain(tall.at[0, back], tks.at[1])
         drain(tall.at[0, back], tks.at[4])
@@ -589,8 +622,9 @@
     elif X > 1:
         drain(lsend.at[0], lrs)
     if Y > 1:
-        drain(xall.at[pl.ds(0, Y - 1), lower], xs.at[4])
-        drain(oy.at[pl.ds(0, Y - 1)], oys)
+        for q in (0, 1):
+            drain(xall.at[pl.ds(0, Y - 1), quarters[q]], xs.at[4 + q])
+        drain(precv.at[pl.ds(0, Y - 1)], oys)
 
     drain(rsum.at[pl.ds(0, Z - 1), 0], rs.at[0])
 
@@ -605,7 +639,14 @@
             drain(kv.at[0, 0], kvs.at[i])
             drain(kv.at[0, 0, pl.ds(0, Z - 1)], kvs.at[i])
 
-    drain(oy.at[0, pl.ds(0, Z - 1)], ozs)
+    @pl.when(owns)
+    def _():
+        drain(rsel.at[pl.ds(0, (Z - 1) * rz // slots)], ozs)
+
+    @pl.when(jnp.logical_not(owns))
+    def _():
+        drain(rsel.at[pl.ds(0, Z * rz // slots)], ozs)
+
 
     @pl.when(keeps)
     def _():
@@ -646,10 +687,12 @@
         pltpu.VMEM((Z, 2, rz, 2 * HD), BF),
         pltpu.VMEM((2, 2, Z, rz, HD), BF),
         pltpu.VMEM((2, rz, HD), BF),
-        pltpu.VMEM((Y, Z, rz, HD), BF),
-        pltpu.VMEM((FB, Y * HD), BF),
-        pltpu.VMEM((R, FB), BF),
-        pltpu.VMEM((R, FB), BF),
+        pltpu.VMEM((rz, HD), BF),
+        pltpu.VMEM((Z // 2 * rz, 2 * HD), BF),
+        pltpu.VMEM((Y * FB, 2 * HD), BF),
+        pltpu.VMEM((Y, Z // 2 * rz, FB), BF),
+        pltpu.VMEM((Y, Z // 2 * rz, FB), BF),
+        pltpu.VMEM((2, Z // 2 * rz, FB), BF),
         pltpu.VMEM((S // 2, slots, FB), BF),
         pltpu.VMEM((X, slots, FX), BF),
         pltpu.VMEM((X, T, FX), BF),
@@ -663,8 +706,8 @@
         pltpu.VMEM((T, FX), F32),
         pltpu.VMEM((S * slots // 128, 128), F32),
         *[dma(()) for _ in range(21)],
-        dma((6,)), dma((6,)), dma((6,)), dma((6,)), dma((2,)), dma((6,)),
-        dma((2,)), dma((2,)), dma((2,)), dma((2,)), dma((Z,)),
+        dma((6,)), dma((6,)), dma((8,)), dma((8,)), dma((2,)), dma((6,)),
+        dma((2,)), dma((2,)), dma((2,)), dma((2,)), dma(()),
     ]
     return pl.pallas_call(
         functools.partial(kernel, dims),

time: 74.9 us -> 72.3 us (0.965)
  Pallas kernels: 73.9 us -> 71.4 us
    pallas_call x1, Pallas kernels: 73.9 us -> 71.4 us  [body(): pl.pallas_call(functools.partial(kernel, dims), out_shape=jax.ShapeDtypeS...]
where the time goes in v5:
time: 72.3 us; the launch traced here: 72.2 us
  Pallas kernels  71.4 us (99%)
  local copies, waits for them, and re-layouts  0.8 us (1%)
    pallas_call x1, Pallas kernels, body(): pl.pallas_call(functools.partial(kernel, dims), out_shape=jax.ShapeDtypeS...  71.4 us

profile of v5, /device:TPU:1, one launch (start us, length us, event | category | flops | bytes accessed | tf_op | source)
XLA Modules:
  0.0 72.2 jit_solution(1811750505566726166)
XLA Ops:
  0.0 71.4 %shard_map.82 = bf16[256,1024]{1,0:T(8,128)(2,1)S(1)} custom-call(bf16[256,1024]{1,0:T(8,128)(2,1)} %tok_any.1, bf16[3,4096,256]{2,1,0:T(8,128)(2,1)} %lin.1, bf16[256,4096]{1,0:T(8,128)(2,1)} %lout.1, bf16[3,64,1024]{2,1,0:T(8,128)(2,1)} %hin_any.1, bf16[64,1024]{1,0:T(8,128)(2,1)} %bitcast.3, s32[32,64]{1,0:T(8,128)} %bitcast.4, s32[32,64]{1,0:T(8,128)} %bitcast.5, ...), custom_call_target="tpu_custom_call" | custom-call | tf_op jit(solution)/shard_map/pallas_call | solution.py:712
  71.4 0.8 %copy.10 = bf16[256,1024]{1,0:T(8,128)(2,1)} copy(bf16[256,1024]{1,0:T(8,128)(2,1)S(1)} %shard_map.82) | data formatting | bytes 1048576
